TPU v7x, 128 devices: a whole 4x4x4 slice. The times are simulated.
128 devices in a mesh: grp: 4 (over y), seq: 32 (over x, z, core).
Axes of the slice: x: 4, y: 4, z: 4, core: 2. Of those that a mesh axis runs over, the one named last changes fastest.
Arguments:
- passage_q: bfloat16 [65536, 4096], P(('grp', 'seq')), may hold values from -8 to 8
- passage_k: bfloat16 [65536, 512], P(('grp', 'seq')), may hold values from -8 to 8
- passage_v: bfloat16 [65536, 512], P(('grp', 'seq')), may hold values from -6 to 6
- kept: int32 [128, 4], P(('grp', 'seq')), may hold values from 0 to 1, as said below
- context_map: int32 [4, 32], P('grp', 'seq'), may hold values from 0 to 127, as said below
- recompute_pos: int32 [4, 2048], P('grp', 'seq'), may hold values from 0 to 16383, as said below
- recompute_q: bfloat16 [4, 2048, 4096], P('grp', 'seq'), may hold values from -8 to 8
- recompute_k: bfloat16 [4, 2048, 512], P('grp', 'seq'), may hold values from -8 to 8
- recompute_v: bfloat16 [4, 2048, 512], P('grp', 'seq'), may hold values from -6 to 6
Outputs:
- passage_out: bfloat16 [65536, 4096], P(('grp', 'seq'))
- reader_out: bfloat16 [4, 2048, 4096], P('grp', 'seq')
Inputs may be any that keep to these rules, and one draw needn't show every extreme that they name: Block 0 of every passage is kept; a passage keeps at most 3 of its 4 blocks, and some passage keeps exactly 3. `context_map`: every passage appears exactly once. Entry [g, s] names a passage encoded on a device whose seq index is s. `recompute_pos`: entries [g, s * 64] to [g, (s + 1) * 64 - 1] are distinct ascending positions from s * 512 to (s + 1) * 512 - 1.
All inputs are finite; a program needn't handle non-finite values.
Results may differ from a plain program's by a relative error of at most 0.005.
Values may be sent and summed in bfloat16 or wider, within the bound.
No kernel may reach another device: no remote copies, remote signals or barrier semaphores. Data moves between devices by JAX's collectives and lax.ppermute only.
A program may use at most 256 MiB of HBM per device.

v0:
```python
import functools
import math

import jax
import jax.numpy as jnp
from jax import lax
from jax.experimental import pallas as pl
from jax.experimental.pallas import tpu as pltpu
from jax.sharding import PartitionSpec as P


HQ = 32
KVH = 4
GQ = HQ // KVH
HD = 128
PLEN = 512
BLK = 128
KEEP = 3
NBLK = PLEN // BLK
R_DEV = 64
N_GRP = 4
N_X = 4
N_Z = 4
N_SEQ = 32
ROW = BLK // 2
META = KEEP * ROW
PIECE = META + 16
KV2 = 2 * HD
QW = GQ * HD + 4 * HD
ROWS = GQ * R_DEV
EXP_SCALE = HD ** (-0.5) * math.log2(math.e)
FAR = 100
STEP = 8
PIECES = N_SEQ


NT = (((1,), (1,)), ((), ()))
bf16 = jnp.bfloat16
f32 = jnp.float32


def seq_of(x, z, c):
    return x * (N_Z * 2) + z * 2 + c


def shift_y(a, k):
    return lax.ppermute(a, "grp", [(i, (i + k) % N_GRP) for i in range(N_GRP)])


def seq_pairs(dx, dz, dc):
    return [
        (seq_of(x, z, c), seq_of((x + dx) % N_X, (z + dz) % N_Z, (c + dc) % 2))
        for x in range(N_X)
        for z in range(N_Z)
        for c in range(2)
    ]


def shift_seq(a, dx=0, dz=0, dc=0):
    return lax.ppermute(a, "seq", seq_pairs(dx, dz, dc))


def place_of():
    s = lax.axis_index("seq")
    return s // (N_Z * 2), lax.rem(s // 2, N_Z), lax.rem(s, 2)


def pack_kernel(half, kept_ref, k_ref, v_ref, out):
    kept = [kept_ref[0, b] for b in range(NBLK)]
    before = [0]
    for b in range(NBLK):
        before.append(before[-1] + kept[b])
    count = before[NBLK]
    row = lax.broadcasted_iota(jnp.int32, (16, HD), 0)
    meta = jnp.where(row == 0, count, FAR)
    for j in range(KEEP):
        block = 0
        for b in range(NBLK):
            block = block + jnp.where((kept[b] > 0) & (before[b] == j), b, 0)
        meta = jnp.where(row == 1 + j, jnp.where(j < count, block, FAR), meta)
        start = pl.multiple_of(block * BLK + half * ROW, ROW)
        for h in range(KVH):
            cols = slice(h * HD, (h + 1) * HD)
            rows = slice(j * ROW, (j + 1) * ROW)
            out[h, rows, :HD] = k_ref[pl.ds(start, ROW), cols]
            out[h, rows, HD:] = v_ref[pl.ds(start, ROW), cols]
    meta = meta.astype(f32).astype(bf16)
    for h in range(KVH):
        out[h, META:, :HD] = meta
        out[h, META:, HD:] = meta


def pack(half, kept, k, v):
    vmem = pl.BlockSpec(memory_space=pltpu.VMEM)
    return pl.pallas_call(
        functools.partial(pack_kernel, half),
        out_shape=jax.ShapeDtypeStruct((KVH, PIECE, KV2), bf16),
        in_specs=[pl.BlockSpec(memory_space=pltpu.SMEM), vmem, vmem],
        out_specs=vmem,
    )(kept, k, v)


def query_kernel(pos_ref, q_ref, rk_ref, rv_ref, q0, q1, q2, q3):
    x, z, c = place_of()
    row = lax.broadcasted_iota(jnp.int32, (R_DEV, R_DEV), 0)
    col = lax.broadcasted_iota(jnp.int32, (R_DEV, R_DEV), 1)
    pos = (pos_ref[...] - seq_of(x, z, c) * PLEN).astype(f32)
    pos = jnp.sum(jnp.where(row == col, pos, 0.0), axis=1, keepdims=True).astype(jnp.int32)
    high = jnp.broadcast_to(pos // 16, (R_DEV, HD)).astype(f32).astype(bf16)
    low = jnp.broadcast_to(pos % 16, (R_DEV, HD)).astype(f32).astype(bf16)
    w = GQ * HD
    for d, out in enumerate((q0, q1, q2, q3)):
        h = lax.rem(x + d, N_X)
        out[:, :w] = q_ref[:, pl.ds(pl.multiple_of(h * w, w), w)]
        cols = pl.ds(pl.multiple_of(h * HD, HD), HD)
        out[:, w : w + HD] = rk_ref[:, cols]
        out[:, w + HD : w + 2 * HD] = rv_ref[:, cols]
        out[:, w + 2 * HD : w + 3 * HD] = high
        out[:, w + 3 * HD :] = low


def split_queries(pos, q, rk, rv):
    query = jax.ShapeDtypeStruct((R_DEV, QW), bf16)
    vmem = pl.BlockSpec(memory_space=pltpu.VMEM)
    return pl.pallas_call(
        query_kernel,
        out_shape=(query,) * N_X,
        in_specs=[vmem] * 4,
        out_specs=(vmem,) * N_X,
        name="queries",
    )(pos, q, rk, rv)


def passage_kernel(q_ref, k_ref, v_ref, o_ref):
    ones = jnp.ones((PLEN, HD), bf16)
    values = jnp.concatenate([v_ref[...], ones], axis=1)
    keys = k_ref[...]
    row = lax.broadcasted_iota(jnp.int32, (BLK, BLK), 0)
    col = lax.broadcasted_iota(jnp.int32, (BLK, BLK), 1)
    hidden = jnp.concatenate([col > row] * GQ, axis=0)
    for i in range(NBLK):
        rows = slice(i * BLK, (i + 1) * BLK)
        n = (i + 1) * BLK
        q = jnp.concatenate([q_ref[rows, g * HD : (g + 1) * HD] for g in range(GQ)], axis=0)
        s = lax.dot_general(q, keys[:n], NT, preferred_element_type=f32)
        last = jnp.where(hidden, -jnp.inf, s[:, n - BLK :])
        s = last if i == 0 else jnp.concatenate([s[:, : n - BLK], last], axis=1)
        m = jnp.max(s, axis=1, keepdims=True)
        p = jnp.exp2((s - m) * EXP_SCALE).astype(bf16)
        mixed = jnp.dot(p, values[:n], preferred_element_type=f32)
        out = (mixed[:, :HD] / mixed[:, HD:]).astype(bf16)
        for g in range(GQ):
            o_ref[rows, g * HD : (g + 1) * HD] = out[g * BLK : (g + 1) * BLK]


def encode(q, k, v, first, heads, done):
    w = GQ * HD
    blocks = [
        pl.BlockSpec((PLEN, w), lambda h: (0, first + h)),
        pl.BlockSpec((PLEN, HD), lambda h: (0, first + h)),
        pl.BlockSpec((PLEN, HD), lambda h: (0, first + h)),
    ]
    operands = [q, k, v]
    if done is not None:
        blocks.append(pl.BlockSpec(memory_space=pl.ANY))
        operands.append(done)

    def kernel(q_ref, k_ref, v_ref, *rest):
        passage_kernel(q_ref, k_ref, v_ref, rest[-1])

    return pl.pallas_call(
        kernel,
        out_shape=jax.ShapeDtypeStruct((PLEN, HQ * HD), bf16),
        grid=(heads,),
        in_specs=blocks,
        out_specs=pl.BlockSpec((PLEN, w), lambda h: (0, first + h)),
        input_output_aliases={} if done is None else {3: 0},
        cost_estimate=pl.CostEstimate(
            flops=heads * 4 * PLEN * PLEN * w,
            bytes_accessed=heads * (9 << 18),
            transcendentals=heads * GQ * PLEN * PLEN,
        ),
    )(*operands)


def reader_kernel(half, *refs):
    arrays = 2 * N_Z
    kv_in, refs = refs[:arrays], refs[arrays:]
    q_in, refs = refs[:N_X], refs[N_X:]
    if half:
        acc_in, state_in = refs[:2]
        outs, refs = refs[2 : 2 + N_X], refs[2 + N_X :]
    else:
        acc_out, state_out = refs[:2]
        refs = refs[2:]
    kv, qs, scores, top, acc, codes, bases, starts, sems = refs
    x, z, c = place_of()
    copies = [
        pltpu.make_async_copy(kv_in[a], kv.at[pl.ds(N_X * a, N_X)], sems.at[N_X + a]) for a in range(arrays)
    ]
    copies += [pltpu.make_async_copy(q_in[d], qs.at[d], sems.at[d]) for d in range(N_X)]
    for copy in copies:
        copy.start()
    for copy in copies:
        copy.wait()

    n = jnp.int32(0)
    for t in range(N_SEQ):
        tx, tz, tc = t // (N_Z * 2), (t // 2) % N_Z, t % 2
        piece = lax.rem(c + tc, 2) * 16 + lax.rem(tz - z + N_Z, N_Z) * 4 + lax.rem(x - tx + N_X, N_X)
        count = jnp.max(kv[piece, META : META + 1, :HD].astype(f32)).astype(jnp.int32)
        starts[t] = n
        for j in range(KEEP):
            codes[n + j] = piece * KEEP + j
            bases[n + j] = t * PLEN
        n = n + count
    starts[N_SEQ] = n
    for j in range(2 * STEP):
        codes[n + j] = 0
        bases[n + j] = FAR * PLEN

    lane = lax.broadcasted_iota(jnp.int32, (1, 2 * ROW), 1)
    w = GQ * HD

    def block(code, cols):
        piece = code // KEEP
        first = pl.multiple_of(lax.rem(code, KEEP) * ROW, ROW)
        return kv[piece, pl.ds(first, ROW), cols]

    def gather(g, count, cols):
        return jnp.concatenate([block(codes[g * STEP + u], cols) for u in range(count * STEP)], axis=0)

    def visit(d, carry):
        shard = seq_of(lax.rem(x - d + N_X, N_X), z, c)
        q = jnp.concatenate([qs[d, :, g * HD : (g + 1) * HD] for g in range(GQ)], axis=0)
        begin = starts[shard]
        end = starts[shard + 1]
        for j in range(KEEP):

            @pl.when(begin + j < end)
            def _():
                number = jnp.max(kv[d, META + 1 + j : META + 2 + j, :HD].astype(f32)).astype(jnp.int32)
                bases[begin + j] = shard * PLEN + number * BLK + half * ROW

        if half:
            old = jnp.broadcast_to(state_in[d, :, 0:1], (ROWS, HD))
        else:
            own_k = jnp.concatenate([qs[d, :, w : w + HD]] * GQ, axis=0).astype(f32)
            own = jnp.sum(q.astype(f32) * own_k, axis=1, keepdims=True) * EXP_SCALE
            old = jnp.broadcast_to(own, (ROWS, HD))
        top[...] = old

        def first_pass(g, count, masked):
            s = lax.dot_general(q, gather(g, count, slice(0, HD)), NT, preferred_element_type=f32)
            best = top[...]
            for u in range(count * STEP // 2):
                part = s[:, u * HD : (u + 1) * HD] * EXP_SCALE
                if masked:
                    b0 = bases[g * STEP + 2 * u]
                    b1 = bases[g * STEP + 2 * u + 1] - ROW
                    spot = (jnp.where(lane < ROW, b0, b1) + lane).astype(f32)
                    high = qs[d, :, w + 2 * HD : w + 3 * HD].astype(f32)
                    place = high * 16 + qs[d, :, w + 3 * HD :].astype(f32)
                    spot = spot - (shard * PLEN).astype(f32)
                    part = jnp.concatenate(
                        [
                            jnp.where(spot < place, part[r * R_DEV : (r + 1) * R_DEV], -jnp.inf)
                            for r in range(GQ)
                        ],
                        axis=0,
                    )
                half_step = STEP // 2
                at = slice((u % half_step) * HD, (u % half_step + 1) * HD)
                scores[g + u // half_step, :, at] = part
                best = jnp.maximum(best, part)
            top[...] = best

        pairs = begin // (2 * STEP)
        groups = (end + STEP - 1) // STEP

        @pl.loop(0, pairs)
        def _(i):
            first_pass(2 * i, 2, False)

        @pl.loop(2 * pairs, groups)
        def _(g):
            first_pass(g, 1, True)

        m = jnp.max(top[...], axis=1, keepdims=True)
        wide = jnp.broadcast_to(m, (ROWS, HD))
        top[...] = wide
        if half:
            alpha = jnp.exp2(old - wide)
            acc[:, :HD] = acc_in[d] * alpha
            acc[:, HD:] = jnp.where(lane == 0, alpha * jnp.broadcast_to(state_in[d, :, ROW : ROW + 1], (ROWS, HD)), 0.0)
        else:
            alpha = jnp.exp2(old - wide).astype(bf16).astype(f32)
            own_v = jnp.concatenate([qs[d, :, w + HD : w + 2 * HD]] * GQ, axis=0).astype(f32)
            acc[:, :HD] = alpha * own_v
            acc[:, HD:] = jnp.where(lane == 0, alpha, 0.0)

        def second_pass(g, count):
            ps = []
            total = acc[:, HD:]
            for u in range(count * STEP // 2):
                half_step = STEP // 2
                at = slice((u % half_step) * HD, (u % half_step + 1) * HD)
                p = jnp.exp2(scores[g + u // half_step, :, at] - top[...]).astype(bf16)
                total = total + p.astype(f32)
                ps.append(p)
            acc[:, HD:] = total
            p = jnp.concatenate(ps, axis=1)
            acc[:, :HD] += jnp.dot(p, gather(g, count, slice(HD, KV2)), preferred_element_type=f32)

        @pl.loop(0, groups // 2)
        def _(i):
            second_pass(2 * i, 2)

        @pl.when(groups % 2 == 1)
        def _():
            second_pass(groups - 1, 1)

        total = jnp.sum(acc[:, HD:], axis=1, keepdims=True)
        if half:
            out = (acc[:, :HD] / total).astype(bf16)
            for e in range(N_X):

                @pl.when(d == e)
                def _():
                    for g in range(GQ):
                        outs[e][:, g * HD : (g + 1) * HD] = out[g * R_DEV : (g + 1) * R_DEV]

        else:
            acc_out[d] = acc[:, :HD]
            state_out[d] = jnp.where(lane < ROW, top[...], total)
        return carry

    lax.fori_loop(0, N_X, visit, 0)


def read(half, kv_arrays, q_arrays, state):
    out = jax.ShapeDtypeStruct((R_DEV, GQ * HD), bf16)
    kept_state = jax.ShapeDtypeStruct((N_X, ROWS, HD), f32)
    arrays = len(kv_arrays)
    hbm = pl.BlockSpec(memory_space=pl.ANY)
    vmem = pl.BlockSpec(memory_space=pltpu.VMEM)
    most = N_SEQ * KEEP
    return pl.pallas_call(
        functools.partial(reader_kernel, half),
        out_shape=(out,) * N_X if half else (kept_state,) * 2,
        in_specs=[hbm] * (arrays + N_X) + [vmem] * len(state),
        out_specs=(vmem,) * (N_X if half else 2),
        scratch_shapes=[
            pltpu.VMEM((PIECES, PIECE, KV2), bf16),
            pltpu.VMEM((N_X, R_DEV, QW), bf16),
            pltpu.VMEM((most // STEP, ROWS, STEP * ROW), f32),
            pltpu.VMEM((ROWS, HD), f32),
            pltpu.VMEM((ROWS, KV2), f32),
            pltpu.SMEM((most + 2 * STEP,), jnp.int32),
            pltpu.SMEM((most + 2 * STEP,), jnp.int32),
            pltpu.SMEM((N_SEQ + 1,), jnp.int32),
            pltpu.SemaphoreType.DMA((N_X + arrays,)),
        ],
        compiler_params=pltpu.CompilerParams(vmem_limit_bytes=40 << 20),
        cost_estimate=pl.CostEstimate(flops=5 << 30, bytes_accessed=8 << 20, transcendentals=6 << 20),
    )(*kv_arrays, *q_arrays, *state)


def around(a, shift):
    return [shift(a, k) for k in (3, 1, 2)]


def whole(
    passage_q,
    passage_k,
    passage_v,
    kept,
    context_map,
    recompute_pos,
    recompute_q,
    recompute_k,
    recompute_v,
):
    y = lax.axis_index("grp")
    x, _, _ = place_of()
    source = context_map[0, 0] // N_SEQ
    rel = (source - y) % N_GRP

    def across_x(own):
        pieces = [lax.dynamic_index_in_dim(own, (x + d) % N_X, 0, keepdims=True) for d in range(N_X)]
        moved = [pieces[0]] + [shift_seq(pieces[d], dx=d) for d in range(1, N_X)]
        return jnp.concatenate(moved, axis=0)

    def choose(offset, own, others):
        up, down, far = others
        return jnp.where(offset == 0, own, jnp.where(offset == 1, up, jnp.where(offset == 2, far, down)))

    def around_z(near):
        up, down, far = around(near, lambda t, k: shift_seq(t, dz=k))
        return [near, up, far, down]

    def swap(t):
        return shift_seq(t, dc=1)

    fence = lax.optimization_barrier
    first = pack(0, kept, passage_k, passage_v)
    near0 = around(first, shift_y)
    second = pack(1, kept, passage_k, passage_v)
    near1 = around(second, shift_y)
    queries = split_queries(recompute_pos, recompute_q[0], recompute_k[0], recompute_v[0])
    q_arrays = [queries[0]] + [shift_seq(queries[d], dx=d) for d in range(1, N_X)]
    passage_out = encode(passage_q, passage_k, passage_v, 0, 2, None)
    rel, passage_out, q_arrays = fence((rel, passage_out, q_arrays))

    mine0 = around_z(across_x(choose(rel, first, near0)))
    other0 = [swap(mine0[0])]
    rel, passage_out, other0 = fence((rel, passage_out, other0))
    passage_out = encode(passage_q, passage_k, passage_v, 2, 2, passage_out)
    rel, passage_out = fence((rel, passage_out))
    mine1 = around_z(across_x(choose(rel, second, near1)))
    kv0 = mine0 + other0 + [swap(t) for t in mine0[1:]]
    state = read(0, kv0, q_arrays, ())
    other1 = [swap(mine1[0])]
    state, other1, far1 = fence((state, other1, mine1[1:]))
    mine1 = mine1[:1] + far1
    kv1 = mine1 + other1 + [swap(t) for t in far1]
    outs = read(1, kv1, q_arrays, state)
    back = [outs[0]] + [shift_seq(outs[d], dx=-d) for d in range(1, N_X)]

    def head(h):
        d = (h - x) % N_X
        return jnp.where(d == 0, back[0], jnp.where(d == 1, back[1], jnp.where(d == 2, back[2], back[3])))

    reader_rows = jnp.concatenate([head(h) for h in range(KVH)], axis=1)
    return (passage_out, reader_rows[None])


def solution(mesh):
    return jax.shard_map(
        whole,
        mesh=mesh,
        in_specs=(
            P(("grp", "seq"), None),
            P(("grp", "seq"), None),
            P(("grp", "seq"), None),
            P(("grp", "seq"), None),
            P("grp", "seq"),
            P("grp", "seq"),
            P("grp", "seq", None),
            P("grp", "seq", None),
            P("grp", "seq", None),
        ),
        out_specs=(P(("grp", "seq"), None), P("grp", "seq", None)),
        check_vma=False,
    )
```

profile of v0, /device:TPU:1, one launch (start us, length us, event | category | flops | bytes accessed | tf_op | source)
XLA Modules:
  0.0 139.2 jit_solution(8999587997890366713)
XLA Ops:
  0.6 2.1 %shard_map.105 = bf16[4,208,256]{2,1,0:T(8,128)(2,1)} custom-call(s32[1,4]{1,0:T(1,128)} %kept_ref.3, bf16[512,512]{1,0:T(8,128)(2,1)} %k_ref.7, bf16[512,512]{1,0:T(8,128)(2,1)} %v_ref.7), custom_call_target="tpu_custom_call" | custom-call | tf_op jit(solution)/shard_map/pallas_call | solution.py:95
  2.7 3.6 %collective-permute-start.3 = (bf16[4,208,256]{2,1,0:T(8,128)(2,1)}, bf16[4,208,256]{2,1,0:T(8,128)(2,1)S(1)}, u32[]{:S(2)}, u32[]{:S(2)}) collective-permute-start(bf16[4,208,256]{2,1,0:T(8,128)(2,1)} %shard_map.105), channel_id=1, source_target_pairs={{0,96},{32,0},{64,32},{96,64},{1,97},{33,1},{65,33},{97,65},{2,98}... | collective-permute-start | bytes 1277960 | tf_op jit(solution)/shard_map/ppermute | solution.py:47
  7.3 2.0 %queries.1 = (bf16[64,1536]{1,0:T(8,128)(2,1)}, bf16[64,1536]{1,0:T(8,128)(2,1)}, bf16[64,1536]{1,0:T(8,128)(2,1)}, bf16[64,1536]{1,0:T(8,128)(2,1)}) custom-call(s32[1,64]{1,0:T(1,128)} %pos_ref.1, bf16[64,4096]{1,0:T(8,128)(2,1)} %bitcast.10, bf16[64,512]{1,0:T(8,128)(2,1)} %bitcast.11, bf16[64,512]{1,0:T(8,128)(2,1)} %bitcast.12), custom_call_target="tpu_custom_call" | custom-call | tf_op jit(solution)/shard_map/queries/pallas_call | solution.py:125
  10.5 2.5 %collective-permute-start.1 = (bf16[64,1536]{1,0:T(8,128)(2,1)}, bf16[64,1536]{1,0:T(8,128)(2,1)S(1)}, u32[]{:S(2)}, u32[]{:S(2)}) collective-permute-start(bf16[64,1536]{1,0:T(8,128)(2,1)} %get-tuple-element.31), channel_id=1, source_target_pairs={{0,16},{1,17},{2,18},{3,19},{4,20},{5,21},{6,22},{7,23},{8,24},{9,... | collective-permute-start | bytes 589832 | tf_op jit(solution)/shard_map/ppermute | solution.py:60
  13.8 1.9 %collective-permute-done.refs_9_ = bf16[64,1536]{1,0:T(8,128)(2,1)S(1)} collective-permute-done((bf16[64,1536]{1,0:T(8,128)(2,1)}, bf16[64,1536]{1,0:T(8,128)(2,1)S(1)}, u32[]{:S(2)}, u32[]{:S(2)}) %collective-permute-start) | collective-permute-done | bytes 196640 | tf_op jit(solution)/shard_map/ppermute | solution.py:60
  15.7 1.3 collective-permute-start.2
  17.0 6.5 %shard_map.104.rest_0_ = bf16[512,4096]{1,0:T(8,128)(2,1)} custom-call(bf16[512,4096]{1,0:T(8,128)(2,1)} %q_ref.3, bf16[512,512]{1,0:T(8,128)(2,1)} %k_ref.7, bf16[512,512]{1,0:T(8,128)(2,1)} %v_ref.7), custom_call_target="tpu_custom_call" | custom-call | flops 2147483648 | bytes 4718592 | tf_op jit(solution)/shard_map/pallas_call | solution.py:171
  24.1 4.8 %collective-permute-done.5 = bf16[4,208,256]{2,1,0:T(8,128)(2,1)S(1)} collective-permute-done((bf16[4,208,256]{2,1,0:T(8,128)(2,1)}, bf16[4,208,256]{2,1,0:T(8,128)(2,1)S(1)}, u32[]{:S(2)}, u32[]{:S(2)}) %collective-permute-start.5) | collective-permute-done | bytes 426016 | tf_op jit(solution)/shard_map/ppermute | solution.py:47
  29.0 2.5 %collective-permute-start.8 = (bf16[1,208,256]{2,1,0:T(8,128)(2,1)S(1)}, bf16[1,208,256]{2,1,0:T(8,128)(2,1)S(1)}, u32[]{:S(2)}, u32[]{:S(2)}) collective-permute-start(bf16[1,208,256]{2,1,0:T(8,128)(2,1)S(1)} %get-tuple-element.65), channel_id=1, source_target_pairs={{0,24},{1,25},{2,26},{3,27},{4,28},{5,29},{6,30},{7,31},{8,0},{9,1... | collective-permute-start | bytes 319496 | tf_op jit(solution)/shard_map/ppermute | solution.py:60
  32.6 2.1 %shard_map.107 = bf16[4,208,256]{2,1,0:T(8,128)(2,1)} custom-call(s32[1,4]{1,0:T(1,128)} %kept_ref.3, bf16[512,512]{1,0:T(8,128)(2,1)} %k_ref.7, bf16[512,512]{1,0:T(8,128)(2,1)} %v_ref.7), custom_call_target="tpu_custom_call" | custom-call | tf_op jit(solution)/shard_map/pallas_call | solution.py:95
  34.7 2.0 %collective-permute-done.7 = bf16[1,208,256]{2,1,0:T(8,128)(2,1)S(1)} collective-permute-done((bf16[1,208,256]{2,1,0:T(8,128)(2,1)S(1)}, bf16[1,208,256]{2,1,0:T(8,128)(2,1)S(1)}, u32[]{:S(2)}, u32[]{:S(2)}) %collective-permute-start.7) | collective-permute-done | bytes 106528 | tf_op jit(solution)/shard_map/ppermute | solution.py:60
  36.7 3.3 %collective-permute-done.6 = bf16[1,208,256]{2,1,0:T(8,128)(2,1)S(1)} collective-permute-done((bf16[1,208,256]{2,1,0:T(8,128)(2,1)S(1)}, bf16[1,208,256]{2,1,0:T(8,128)(2,1)S(1)}, u32[]{:S(2)}, u32[]{:S(2)}) %collective-permute-start.6) | collective-permute-done | bytes 106528 | tf_op jit(solution)/shard_map/ppermute | solution.py:60
  40.8 3.8 %collective-permute-start.16 = (bf16[4,208,256]{2,1,0:T(8,128)(2,1)S(1)}, bf16[4,208,256]{2,1,0:T(8,128)(2,1)S(1)}, u32[]{:S(2)}, u32[]{:S(2)}) collective-permute-start(bf16[4,208,256]{2,1,0:T(8,128)(2,1)S(1)} %pad_maximum_fusion.refs_0_), channel_id=1, source_target_pairs={{0,6},{1,7},{2,0},{3,1},{4,2},{5,3},{6,4},{7,5},{8,14},{9,15},{10,... | collective-permute-start | bytes 1277960 | tf_op jit(solution)/shard_map/ppermute | solution.py:60
  46.5 6.5 %shard_map.106 = bf16[512,4096]{1,0:T(8,128)(2,1)} custom-call(bf16[512,4096]{1,0:T(8,128)(2,1)} %q_ref.3, bf16[512,512]{1,0:T(8,128)(2,1)} %k_ref.7, bf16[512,512]{1,0:T(8,128)(2,1)} %v_ref.7, bf16[512,4096]{1,0:T(8,128)(2,1)} %shard_map.104.rest_0_), custom_call_target="tpu_custom_call", output_to_operand_aliasing={{}: (3, {})} | custom-call | flops 2147483648 | bytes 4718592 | tf_op jit(solution)/shard_map/pallas_call | solution.py:171
  53.0 9.8 %collective-permute-done.16.refs_1_ = bf16[4,208,256]{2,1,0:T(8,128)(2,1)S(1)} collective-permute-done((bf16[4,208,256]{2,1,0:T(8,128)(2,1)S(1)}, bf16[4,208,256]{2,1,0:T(8,128)(2,1)S(1)}, u32[]{:S(2)}, u32[]{:S(2)}) %collective-permute-start.16) | collective-permute-done | bytes 426016 | tf_op jit(solution)/shard_map/ppermute | solution.py:60
  63.8 2.7 %collective-permute-done.18.refs_3_ = bf16[4,208,256]{2,1,0:T(8,128)(2,1)S(1)} collective-permute-done((bf16[4,208,256]{2,1,0:T(8,128)(2,1)S(1)}, bf16[4,208,256]{2,1,0:T(8,128)(2,1)S(1)}, u32[]{:S(2)}, u32[]{:S(2)}) %collective-permute-start.18) | collective-permute-done | bytes 426016 | tf_op jit(solution)/shard_map/ppermute | solution.py:60
  68.0 1.2 select_select_fusion
  69.3 1.8 %collective-permute-start.15 = (bf16[1,208,256]{2,1,0:T(8,128)(2,1)S(1)}, bf16[1,208,256]{2,1,0:T(8,128)(2,1)S(1)}, u32[]{:S(2)}, u32[]{:S(2)}) collective-permute-start(bf16[1,208,256]{2,1,0:T(8,128)(2,1)S(1)} %get-tuple-element.61), channel_id=1, source_target_pairs={{0,24},{1,25},{2,26},{3,27},{4,28},{5,29},{6,30},{7,31},{8,0},{9,1... | collective-permute-start | bytes 319496 | tf_op jit(solution)/shard_map/ppermute | solution.py:60
  71.0 1.2 collective-permute-start.14
  72.3 1.2 collective-permute-done.15
  74.5 1.6 %collective-permute-done.14 = bf16[1,208,256]{2,1,0:T(8,128)(2,1)S(1)} collective-permute-done((bf16[1,208,256]{2,1,0:T(8,128)(2,1)S(1)}, bf16[1,208,256]{2,1,0:T(8,128)(2,1)S(1)}, u32[]{:S(2)}, u32[]{:S(2)}) %collective-permute-start.14) | collective-permute-done | bytes 106528 | tf_op jit(solution)/shard_map/ppermute | solution.py:60
  76.1 2.7 %collective-permute-done.13 = bf16[1,208,256]{2,1,0:T(8,128)(2,1)S(1)} collective-permute-done((bf16[1,208,256]{2,1,0:T(8,128)(2,1)S(1)}, bf16[1,208,256]{2,1,0:T(8,128)(2,1)S(1)}, u32[]{:S(2)}, u32[]{:S(2)}) %collective-permute-start.13) | collective-permute-done | bytes 106528 | tf_op jit(solution)/shard_map/ppermute | solution.py:60
  78.8 4.2 %collective-permute-start.22 = (bf16[4,208,256]{2,1,0:T(8,128)(2,1)S(1)}, bf16[4,208,256]{2,1,0:T(8,128)(2,1)S(1)}, u32[]{:S(2)}, u32[]{:S(2)}) collective-permute-start(bf16[4,208,256]{2,1,0:T(8,128)(2,1)S(1)} %pad_maximum_fusion.1.refs_0_), channel_id=1, source_target_pairs={{0,1},{1,0},{2,3},{3,2},{4,5},{5,4},{6,7},{7,6},{8,9},{9,8},{10,11... | collective-permute-start | bytes 1277960 | tf_op jit(solution)/shard_map/ppermute | solution.py:60
  83.0 3.8 %collective-permute-start.23 = (bf16[4,208,256]{2,1,0:T(8,128)(2,1)S(1)}, bf16[4,208,256]{2,1,0:T(8,128)(2,1)S(1)}, u32[]{:S(2)}, u32[]{:S(2)}) collective-permute-start(bf16[4,208,256]{2,1,0:T(8,128)(2,1)S(1)} %pad_maximum_fusion.1.refs_0_), channel_id=1, source_target_pairs={{0,6},{1,7},{2,0},{3,1},{4,2},{5,3},{6,4},{7,5},{8,14},{9,15},{10,... | collective-permute-start | bytes 1277960 | tf_op jit(solution)/shard_map/ppermute | solution.py:60
  87.5 14.7 %shard_map.108 = (f32[4,512,128]{2,1,0:T(8,128)S(1)}, f32[4,512,128]{2,1,0:T(8,128)S(1)}) custom-call(bf16[4,208,256]{2,1,0:T(8,128)(2,1)S(1)} %pad_maximum_fusion.refs_0_, bf16[4,208,256]{2,1,0:T(8,128)(2,1)S(1)} %collective-permute-done.16.refs_1_, bf16[4,208,256]{2,1,0:T(8,128)(2,1)S(1)} %collective-permute-done.17.refs_2_, ...), custom_call_target="tpu_custom_call" | custom-call | flops 5368709120 | bytes 8388608 | tf_op jit(solution)/shard_map/pallas_call | solution.py:348
  102.2 2.8 %collective-permute-done.23.refs_1_ = bf16[4,208,256]{2,1,0:T(8,128)(2,1)S(1)} collective-permute-done((bf16[4,208,256]{2,1,0:T(8,128)(2,1)S(1)}, bf16[4,208,256]{2,1,0:T(8,128)(2,1)S(1)}, u32[]{:S(2)}, u32[]{:S(2)}) %collective-permute-start.23) | collective-permute-done | bytes 426016 | tf_op jit(solution)/shard_map/ppermute | solution.py:60
  105.0 3.7 %collective-permute-done.25.refs_3_ = bf16[4,208,256]{2,1,0:T(8,128)(2,1)S(1)} collective-permute-done((bf16[4,208,256]{2,1,0:T(8,128)(2,1)S(1)}, bf16[4,208,256]{2,1,0:T(8,128)(2,1)S(1)}, u32[]{:S(2)}, u32[]{:S(2)}) %collective-permute-start.25) | collective-permute-done | bytes 426016 | tf_op jit(solution)/shard_map/ppermute | solution.py:60
  112.0 15.3 %shard_map.109 = (bf16[64,1024]{1,0:T(8,128)(2,1)S(1)}, bf16[64,1024]{1,0:T(8,128)(2,1)S(1)}, bf16[64,1024]{1,0:T(8,128)(2,1)S(1)}, bf16[64,1024]{1,0:T(8,128)(2,1)S(1)}) custom-call(bf16[4,208,256]{2,1,0:T(8,128)(2,1)S(1)} %pad_maximum_fusion.1.refs_0_, bf16[4,208,256]{2,1,0:T(8,128)(2,1)S(1)} %collective-permute-done.23.refs_1_, ...), custom_call_target="tpu_custom_call" | custom-call | flops 5368709120 | bytes 8388608 | tf_op jit(solution)/shard_map/pallas_call | solution.py:348
  127.4 1.8 %collective-permute-start.29 = (bf16[64,1024]{1,0:T(8,128)(2,1)S(1)}, bf16[64,1024]{1,0:T(8,128)(2,1)S(1)}, u32[]{:S(2)}, u32[]{:S(2)}) collective-permute-start(bf16[64,1024]{1,0:T(8,128)(2,1)S(1)} %get-tuple-element.53), channel_id=1, source_target_pairs={{0,24},{1,25},{2,26},{3,27},{4,28},{5,29},{6,30},{7,31},{8,0},{9,1... | collective-permute-start | bytes 393224 | tf_op jit(solution)/shard_map/ppermute | solution.py:60
  129.8 2.1 %collective-permute-done.29 = bf16[64,1024]{1,0:T(8,128)(2,1)S(1)} collective-permute-done((bf16[64,1024]{1,0:T(8,128)(2,1)S(1)}, bf16[64,1024]{1,0:T(8,128)(2,1)S(1)}, u32[]{:S(2)}, u32[]{:S(2)}) %collective-permute-start.29) | collective-permute-done | bytes 131104 | tf_op jit(solution)/shard_map/ppermute | solution.py:60
  131.9 3.1 %collective-permute-done.30 = bf16[64,1024]{1,0:T(8,128)(2,1)S(1)} collective-permute-done((bf16[64,1024]{1,0:T(8,128)(2,1)S(1)}, bf16[64,1024]{1,0:T(8,128)(2,1)S(1)}, u32[]{:S(2)}, u32[]{:S(2)}) %collective-permute-start.30) | collective-permute-done | bytes 131104 | tf_op jit(solution)/shard_map/ppermute | solution.py:60
  134.9 3.4 %collective-permute-done.31 = bf16[64,1024]{1,0:T(8,128)(2,1)S(1)} collective-permute-done((bf16[64,1024]{1,0:T(8,128)(2,1)S(1)}, bf16[64,1024]{1,0:T(8,128)(2,1)S(1)}, u32[]{:S(2)}, u32[]{:S(2)}) %collective-permute-start.31) | collective-permute-done | bytes 131104 | tf_op jit(solution)/shard_map/ppermute | solution.py:60
  (53 shorter events, 16.1 us)
Async XLA Ops:
  2.7 21.4 %collective-permute-start.3 = (bf16[4,208,256]{2,1,0:T(8,128)(2,1)}, bf16[4,208,256]{2,1,0:T(8,128)(2,1)S(1)}, u32[]{:S(2)}, u32[]{:S(2)}) collective-permute-start(bf16[4,208,256]{2,1,0:T(8,128)(2,1)} %shard_map.105), channel_id=1, source_target_pairs={{0,96},{32,0},{64,32},{96,64},{1,97},{33,1},{65,33},{97,65},{2,98}... | collective-permute-start | bytes 1277960 | tf_op jit(solution)/shard_map/ppermute | solution.py:47
  6.2 17.8 %collective-permute-start.4 = (bf16[4,208,256]{2,1,0:T(8,128)(2,1)}, bf16[4,208,256]{2,1,0:T(8,128)(2,1)S(1)}, u32[]{:S(2)}, u32[]{:S(2)}) collective-permute-start(bf16[4,208,256]{2,1,0:T(8,128)(2,1)} %shard_map.105), channel_id=1, source_target_pairs={{0,64},{32,96},{64,0},{96,32},{1,65},{33,97},{65,1},{97,33},{2,66}... | collective-permute-start | bytes 1277960 | tf_op jit(solution)/shard_map/ppermute | solution.py:47
  6.6 22.2 %collective-permute-start.5 = (bf16[4,208,256]{2,1,0:T(8,128)(2,1)}, bf16[4,208,256]{2,1,0:T(8,128)(2,1)S(1)}, u32[]{:S(2)}, u32[]{:S(2)}) collective-permute-start(bf16[4,208,256]{2,1,0:T(8,128)(2,1)} %shard_map.105), channel_id=1, source_target_pairs={{0,32},{32,64},{64,96},{96,0},{1,33},{33,65},{65,97},{97,1},{2,34}... | collective-permute-start | bytes 1277960 | tf_op jit(solution)/shard_map/ppermute | solution.py:47
  9.3 6.4 %collective-permute-start = (bf16[64,1536]{1,0:T(8,128)(2,1)}, bf16[64,1536]{1,0:T(8,128)(2,1)S(1)}, u32[]{:S(2)}, u32[]{:S(2)}) collective-permute-start(bf16[64,1536]{1,0:T(8,128)(2,1)} %get-tuple-element.30), channel_id=1, source_target_pairs={{0,8},{1,9},{2,10},{3,11},{4,12},{5,13},{6,14},{7,15},{8,16},{9,17... | collective-permute-start | bytes 589832 | tf_op jit(solution)/shard_map/ppermute | solution.py:60
  10.5 12.9 %collective-permute-start.1 = (bf16[64,1536]{1,0:T(8,128)(2,1)}, bf16[64,1536]{1,0:T(8,128)(2,1)S(1)}, u32[]{:S(2)}, u32[]{:S(2)}) collective-permute-start(bf16[64,1536]{1,0:T(8,128)(2,1)} %get-tuple-element.31), channel_id=1, source_target_pairs={{0,16},{1,17},{2,18},{3,19},{4,20},{5,21},{6,22},{7,23},{8,24},{9,... | collective-permute-start | bytes 589832 | tf_op jit(solution)/shard_map/ppermute | solution.py:60
  15.7 7.7 %collective-permute-start.2 = (bf16[64,1536]{1,0:T(8,128)(2,1)}, bf16[64,1536]{1,0:T(8,128)(2,1)S(1)}, u32[]{:S(2)}, u32[]{:S(2)}) collective-permute-start(bf16[64,1536]{1,0:T(8,128)(2,1)} %get-tuple-element.32), channel_id=1, source_target_pairs={{0,24},{1,25},{2,26},{3,27},{4,28},{5,29},{6,30},{7,31},{8,0},{9,1... | collective-permute-start | bytes 589832 | tf_op jit(solution)/shard_map/ppermute | solution.py:60
  29.0 5.7 %collective-permute-start.8 = (bf16[1,208,256]{2,1,0:T(8,128)(2,1)S(1)}, bf16[1,208,256]{2,1,0:T(8,128)(2,1)S(1)}, u32[]{:S(2)}, u32[]{:S(2)}) collective-permute-start(bf16[1,208,256]{2,1,0:T(8,128)(2,1)S(1)} %get-tuple-element.65), channel_id=1, source_target_pairs={{0,24},{1,25},{2,26},{3,27},{4,28},{5,29},{6,30},{7,31},{8,0},{9,1... | collective-permute-start | bytes 319496 | tf_op jit(solution)/shard_map/ppermute | solution.py:60
  31.5 5.2 %collective-permute-start.7 = (bf16[1,208,256]{2,1,0:T(8,128)(2,1)S(1)}, bf16[1,208,256]{2,1,0:T(8,128)(2,1)S(1)}, u32[]{:S(2)}, u32[]{:S(2)}) collective-permute-start(bf16[1,208,256]{2,1,0:T(8,128)(2,1)S(1)} %get-tuple-element.66), channel_id=1, source_target_pairs={{0,16},{1,17},{2,18},{3,19},{4,20},{5,21},{6,22},{7,23},{8,24},{9,... | collective-permute-start | bytes 319496 | tf_op jit(solution)/shard_map/ppermute | solution.py:60
  32.0 7.9 %collective-permute-start.6 = (bf16[1,208,256]{2,1,0:T(8,128)(2,1)S(1)}, bf16[1,208,256]{2,1,0:T(8,128)(2,1)S(1)}, u32[]{:S(2)}, u32[]{:S(2)}) collective-permute-start(bf16[1,208,256]{2,1,0:T(8,128)(2,1)S(1)} %get-tuple-element.67), channel_id=1, source_target_pairs={{0,8},{1,9},{2,10},{3,11},{4,12},{5,13},{6,14},{7,15},{8,16},{9,17... | collective-permute-start | bytes 319496 | tf_op jit(solution)/shard_map/ppermute | solution.py:60
  34.7 10.6 %collective-permute-start.10 = (bf16[4,208,256]{2,1,0:T(8,128)(2,1)}, bf16[4,208,256]{2,1,0:T(8,128)(2,1)}, u32[]{:S(2)}, u32[]{:S(2)}) collective-permute-start(bf16[4,208,256]{2,1,0:T(8,128)(2,1)} %shard_map.107), channel_id=1, source_target_pairs={{0,96},{32,0},{64,32},{96,64},{1,97},{33,1},{65,33},{97,65},{2,98}... | collective-permute-start | bytes 1277960 | tf_op jit(solution)/shard_map/ppermute | solution.py:47
  40.0 5.6 %collective-permute-start.9 = (bf16[4,208,256]{2,1,0:T(8,128)(2,1)S(1)}, bf16[4,208,256]{2,1,0:T(8,128)(2,1)S(1)}, u32[]{:S(2)}, u32[]{:S(2)}) collective-permute-start(bf16[4,208,256]{2,1,0:T(8,128)(2,1)S(1)} %pad_maximum_fusion.refs_0_), channel_id=1, source_target_pairs={{0,1},{1,0},{2,3},{3,2},{4,5},{5,4},{6,7},{7,6},{8,9},{9,8},{10,11... | collective-permute-start | bytes 1277960 | tf_op jit(solution)/shard_map/ppermute | solution.py:60
  40.8 22.0 %collective-permute-start.16 = (bf16[4,208,256]{2,1,0:T(8,128)(2,1)S(1)}, bf16[4,208,256]{2,1,0:T(8,128)(2,1)S(1)}, u32[]{:S(2)}, u32[]{:S(2)}) collective-permute-start(bf16[4,208,256]{2,1,0:T(8,128)(2,1)S(1)} %pad_maximum_fusion.refs_0_), channel_id=1, source_target_pairs={{0,6},{1,7},{2,0},{3,1},{4,2},{5,3},{6,4},{7,5},{8,14},{9,15},{10,... | collective-permute-start | bytes 1277960 | tf_op jit(solution)/shard_map/ppermute | solution.py:60
  44.6 19.2 %collective-permute-start.17 = (bf16[4,208,256]{2,1,0:T(8,128)(2,1)S(1)}, bf16[4,208,256]{2,1,0:T(8,128)(2,1)S(1)}, u32[]{:S(2)}, u32[]{:S(2)}) collective-permute-start(bf16[4,208,256]{2,1,0:T(8,128)(2,1)S(1)} %pad_maximum_fusion.refs_0_), channel_id=1, source_target_pairs={{0,4},{1,5},{2,6},{3,7},{4,0},{5,1},{6,2},{7,3},{8,12},{9,13},{10,... | collective-permute-start | bytes 1277960 | tf_op jit(solution)/shard_map/ppermute | solution.py:60
  44.6 21.9 %collective-permute-start.18 = (bf16[4,208,256]{2,1,0:T(8,128)(2,1)S(1)}, bf16[4,208,256]{2,1,0:T(8,128)(2,1)S(1)}, u32[]{:S(2)}, u32[]{:S(2)}) collective-permute-start(bf16[4,208,256]{2,1,0:T(8,128)(2,1)S(1)} %pad_maximum_fusion.refs_0_), channel_id=1, source_target_pairs={{0,2},{1,3},{2,4},{3,5},{4,6},{5,7},{6,0},{7,1},{8,10},{9,11},{10,... | collective-permute-start | bytes 1277960 | tf_op jit(solution)/shard_map/ppermute | solution.py:60
  45.3 21.9 %collective-permute-start.11 = (bf16[4,208,256]{2,1,0:T(8,128)(2,1)}, bf16[4,208,256]{2,1,0:T(8,128)(2,1)}, u32[]{:S(2)}, u32[]{:S(2)}) collective-permute-start(bf16[4,208,256]{2,1,0:T(8,128)(2,1)} %shard_map.107), channel_id=1, source_target_pairs={{0,64},{32,96},{64,0},{96,32},{1,65},{33,97},{65,1},{97,33},{2,66}... | collective-permute-start | bytes 1277960 | tf_op jit(solution)/shard_map/ppermute | solution.py:47
  45.7 22.3 %collective-permute-start.12 = (bf16[4,208,256]{2,1,0:T(8,128)(2,1)}, bf16[4,208,256]{2,1,0:T(8,128)(2,1)}, u32[]{:S(2)}, u32[]{:S(2)}) collective-permute-start(bf16[4,208,256]{2,1,0:T(8,128)(2,1)} %shard_map.107), channel_id=1, source_target_pairs={{0,32},{32,64},{64,96},{96,0},{1,33},{33,65},{65,97},{97,1},{2,34}... | collective-permute-start | bytes 1277960 | tf_op jit(solution)/shard_map/ppermute | solution.py:47
  62.8 23.9 %collective-permute-start.19 = (bf16[4,208,256]{2,1,0:T(8,128)(2,1)S(1)}, bf16[4,208,256]{2,1,0:T(8,128)(2,1)S(1)}, u32[]{:S(2)}, u32[]{:S(2)}) collective-permute-start(bf16[4,208,256]{2,1,0:T(8,128)(2,1)S(1)} %collective-permute-done.16.refs_1_), channel_id=1, source_target_pairs={{0,1},{1,0},{2,3},{3,2},{4,5},{5,4},{6,7},{7,6},{8,9},{9,8},{10,11... | collective-permute-start | bytes 1277960 | tf_op jit(solution)/shard_map/ppermute | solution.py:60
  63.8 23.0 %collective-permute-start.20 = (bf16[4,208,256]{2,1,0:T(8,128)(2,1)S(1)}, bf16[4,208,256]{2,1,0:T(8,128)(2,1)S(1)}, u32[]{:S(2)}, u32[]{:S(2)}) collective-permute-start(bf16[4,208,256]{2,1,0:T(8,128)(2,1)S(1)} %collective-permute-done.17.refs_2_), channel_id=1, source_target_pairs={{0,1},{1,0},{2,3},{3,2},{4,5},{5,4},{6,7},{7,6},{8,9},{9,8},{10,11... | collective-permute-start | bytes 1277960 | tf_op jit(solution)/shard_map/ppermute | solution.py:60
  66.5 21.0 %collective-permute-start.21 = (bf16[4,208,256]{2,1,0:T(8,128)(2,1)S(1)}, bf16[4,208,256]{2,1,0:T(8,128)(2,1)S(1)}, u32[]{:S(2)}, u32[]{:S(2)}) collective-permute-start(bf16[4,208,256]{2,1,0:T(8,128)(2,1)S(1)} %collective-permute-done.18.refs_3_), channel_id=1, source_target_pairs={{0,1},{1,0},{2,3},{3,2},{4,5},{5,4},{6,7},{7,6},{8,9},{9,8},{10,11... | collective-permute-start | bytes 1277960 | tf_op jit(solution)/shard_map/ppermute | solution.py:60
  69.3 4.2 %collective-permute-start.15 = (bf16[1,208,256]{2,1,0:T(8,128)(2,1)S(1)}, bf16[1,208,256]{2,1,0:T(8,128)(2,1)S(1)}, u32[]{:S(2)}, u32[]{:S(2)}) collective-permute-start(bf16[1,208,256]{2,1,0:T(8,128)(2,1)S(1)} %get-tuple-element.61), channel_id=1, source_target_pairs={{0,24},{1,25},{2,26},{3,27},{4,28},{5,29},{6,30},{7,31},{8,0},{9,1... | collective-permute-start | bytes 319496 | tf_op jit(solution)/shard_map/ppermute | solution.py:60
  71.0 5.1 %collective-permute-start.14 = (bf16[1,208,256]{2,1,0:T(8,128)(2,1)S(1)}, bf16[1,208,256]{2,1,0:T(8,128)(2,1)S(1)}, u32[]{:S(2)}, u32[]{:S(2)}) collective-permute-start(bf16[1,208,256]{2,1,0:T(8,128)(2,1)S(1)} %get-tuple-element.62), channel_id=1, source_target_pairs={{0,16},{1,17},{2,18},{3,19},{4,20},{5,21},{6,22},{7,23},{8,24},{9,... | collective-permute-start | bytes 319496 | tf_op jit(solution)/shard_map/ppermute | solution.py:60
  73.5 5.3 %collective-permute-start.13 = (bf16[1,208,256]{2,1,0:T(8,128)(2,1)S(1)}, bf16[1,208,256]{2,1,0:T(8,128)(2,1)S(1)}, u32[]{:S(2)}, u32[]{:S(2)}) collective-permute-start(bf16[1,208,256]{2,1,0:T(8,128)(2,1)S(1)} %get-tuple-element.63), channel_id=1, source_target_pairs={{0,8},{1,9},{2,10},{3,11},{4,12},{5,13},{6,14},{7,15},{8,16},{9,17... | collective-permute-start | bytes 319496 | tf_op jit(solution)/shard_map/ppermute | solution.py:60
  78.8 23.3 %collective-permute-start.22 = (bf16[4,208,256]{2,1,0:T(8,128)(2,1)S(1)}, bf16[4,208,256]{2,1,0:T(8,128)(2,1)S(1)}, u32[]{:S(2)}, u32[]{:S(2)}) collective-permute-start(bf16[4,208,256]{2,1,0:T(8,128)(2,1)S(1)} %pad_maximum_fusion.1.refs_0_), channel_id=1, source_target_pairs={{0,1},{1,0},{2,3},{3,2},{4,5},{5,4},{6,7},{7,6},{8,9},{9,8},{10,11... | collective-permute-start | bytes 1277960 | tf_op jit(solution)/shard_map/ppermute | solution.py:60
  83.0 22.0 %collective-permute-start.23 = (bf16[4,208,256]{2,1,0:T(8,128)(2,1)S(1)}, bf16[4,208,256]{2,1,0:T(8,128)(2,1)S(1)}, u32[]{:S(2)}, u32[]{:S(2)}) collective-permute-start(bf16[4,208,256]{2,1,0:T(8,128)(2,1)S(1)} %pad_maximum_fusion.1.refs_0_), channel_id=1, source_target_pairs={{0,6},{1,7},{2,0},{3,1},{4,2},{5,3},{6,4},{7,5},{8,14},{9,15},{10,... | collective-permute-start | bytes 1277960 | tf_op jit(solution)/shard_map/ppermute | solution.py:60
  86.8 18.2 %collective-permute-start.24 = (bf16[4,208,256]{2,1,0:T(8,128)(2,1)S(1)}, bf16[4,208,256]{2,1,0:T(8,128)(2,1)S(1)}, u32[]{:S(2)}, u32[]{:S(2)}) collective-permute-start(bf16[4,208,256]{2,1,0:T(8,128)(2,1)S(1)} %pad_maximum_fusion.1.refs_0_), channel_id=1, source_target_pairs={{0,4},{1,5},{2,6},{3,7},{4,0},{5,1},{6,2},{7,3},{8,12},{9,13},{10,... | collective-permute-start | bytes 1277960 | tf_op jit(solution)/shard_map/ppermute | solution.py:60
  86.8 21.9 %collective-permute-start.25 = (bf16[4,208,256]{2,1,0:T(8,128)(2,1)S(1)}, bf16[4,208,256]{2,1,0:T(8,128)(2,1)S(1)}, u32[]{:S(2)}, u32[]{:S(2)}) collective-permute-start(bf16[4,208,256]{2,1,0:T(8,128)(2,1)S(1)} %pad_maximum_fusion.1.refs_0_), channel_id=1, source_target_pairs={{0,2},{1,3},{2,4},{3,5},{4,6},{5,7},{6,0},{7,1},{8,10},{9,11},{10,... | collective-permute-start | bytes 1277960 | tf_op jit(solution)/shard_map/ppermute | solution.py:60
  108.7 2.1 %collective-permute-start.26 = (bf16[4,208,256]{2,1,0:T(8,128)(2,1)S(1)}, bf16[4,208,256]{2,1,0:T(8,128)(2,1)S(1)}, u32[]{:S(2)}, u32[]{:S(2)}) collective-permute-start(bf16[4,208,256]{2,1,0:T(8,128)(2,1)S(1)} %collective-permute-done.23.refs_1_), channel_id=1, source_target_pairs={{0,1},{1,0},{2,3},{3,2},{4,5},{5,4},{6,7},{7,6},{8,9},{9,8},{10,11... | collective-permute-start | bytes 1277960 | tf_op jit(solution)/shard_map/ppermute | solution.py:60
  109.4 2.0 %collective-permute-start.27 = (bf16[4,208,256]{2,1,0:T(8,128)(2,1)S(1)}, bf16[4,208,256]{2,1,0:T(8,128)(2,1)S(1)}, u32[]{:S(2)}, u32[]{:S(2)}) collective-permute-start(bf16[4,208,256]{2,1,0:T(8,128)(2,1)S(1)} %collective-permute-done.24.refs_2_), channel_id=1, source_target_pairs={{0,1},{1,0},{2,3},{3,2},{4,5},{5,4},{6,7},{7,6},{8,9},{9,8},{10,11... | collective-permute-start | bytes 1277960 | tf_op jit(solution)/shard_map/ppermute | solution.py:60
  109.4 2.6 %collective-permute-start.28 = (bf16[4,208,256]{2,1,0:T(8,128)(2,1)S(1)}, bf16[4,208,256]{2,1,0:T(8,128)(2,1)S(1)}, u32[]{:S(2)}, u32[]{:S(2)}) collective-permute-start(bf16[4,208,256]{2,1,0:T(8,128)(2,1)S(1)} %collective-permute-done.25.refs_3_), channel_id=1, source_target_pairs={{0,1},{1,0},{2,3},{3,2},{4,5},{5,4},{6,7},{7,6},{8,9},{9,8},{10,11... | collective-permute-start | bytes 1277960 | tf_op jit(solution)/shard_map/ppermute | solution.py:60
  127.4 4.5 %collective-permute-start.29 = (bf16[64,1024]{1,0:T(8,128)(2,1)S(1)}, bf16[64,1024]{1,0:T(8,128)(2,1)S(1)}, u32[]{:S(2)}, u32[]{:S(2)}) collective-permute-start(bf16[64,1024]{1,0:T(8,128)(2,1)S(1)} %get-tuple-element.53), channel_id=1, source_target_pairs={{0,24},{1,25},{2,26},{3,27},{4,28},{5,29},{6,30},{7,31},{8,0},{9,1... | collective-permute-start | bytes 393224 | tf_op jit(solution)/shard_map/ppermute | solution.py:60
  129.2 5.8 %collective-permute-start.30 = (bf16[64,1024]{1,0:T(8,128)(2,1)S(1)}, bf16[64,1024]{1,0:T(8,128)(2,1)S(1)}, u32[]{:S(2)}, u32[]{:S(2)}) collective-permute-start(bf16[64,1024]{1,0:T(8,128)(2,1)S(1)} %get-tuple-element.54), channel_id=1, source_target_pairs={{0,16},{1,17},{2,18},{3,19},{4,20},{5,21},{6,22},{7,23},{8,24},{9,... | collective-permute-start | bytes 393224 | tf_op jit(solution)/shard_map/ppermute | solution.py:60
  129.2 9.1 %collective-permute-start.31 = (bf16[64,1024]{1,0:T(8,128)(2,1)S(1)}, bf16[64,1024]{1,0:T(8,128)(2,1)S(1)}, u32[]{:S(2)}, u32[]{:S(2)}) collective-permute-start(bf16[64,1024]{1,0:T(8,128)(2,1)S(1)} %get-tuple-element.55), channel_id=1, source_target_pairs={{0,8},{1,9},{2,10},{3,11},{4,12},{5,13},{6,14},{7,15},{8,16},{9,17... | collective-permute-start | bytes 393224 | tf_op jit(solution)/shard_map/ppermute | solution.py:60
  (3 other events, 88.6 us)
where the time goes:
time: 140 us; the launch traced here: 139 us
  Pallas kernels  49.1 us (35%)
  waiting for transfers between devices  48.5 us (35%)
  starting transfers between devices  37.7 us (27%)
  other arithmetic  2.3 us (2%)
  between operations  1.53 us (1%)
    ppermute x26, waiting for transfers between devices, shift_seq(): return lax.ppermute(a, 'seq', seq_pairs(dx, dz, dc))  42.3 us
    ppermute x26, starting transfers between devices, shift_seq(): return lax.ppermute(a, 'seq', seq_pairs(dx, dz, dc))  31.9 us
    pallas_call x2, Pallas kernels, read(): pl.pallas_call(functools.partial(reader_kernel, half), out_shape=(out,) *...  30 us
    pallas_call x2, Pallas kernels, encode(): pl.pallas_call(kernel, out_shape=jax.ShapeDtypeStruct((PLEN, HQ * HD), bf...  12.9 us
    ppermute x6, waiting for transfers between devices, shift_y(): return lax.ppermute(a, 'grp', [(i, (i + k) % N_GRP) for i in range(N_GRP)])  6.2 us
    ppermute x6, starting transfers between devices, shift_y(): return lax.ppermute(a, 'grp', [(i, (i + k) % N_GRP) for i in range(N_GRP)])  5.82 us
    pallas_call x2, Pallas kernels, pack(): pl.pallas_call(functools.partial(pack_kernel, half), out_shape=jax.ShapeD...  4.13 us
  transfers between devices with their start and end apart: 32, of which 19 were waited for; matrix products, arithmetic and copies ran while one was open for 1% of the time, Pallas kernels for 23%

commit v1 on v0

--- a/solution.py
+++ b/solution.py
@@ -188,17 +188,19 @@
     kv_in, refs = refs[:arrays], refs[arrays:]
     q_in, refs = refs[:N_X], refs[N_X:]
     if half:
-        acc_in, state_in = refs[:2]
+        mixes, stats = refs[:2]
         outs, refs = refs[2 : 2 + N_X], refs[2 + N_X :]
     else:
-        acc_out, state_out = refs[:2]
+        mixes, stats = refs[:2]
         refs = refs[2:]
-    kv, qs, scores, top, acc, codes, bases, starts, sems = refs
+    kv, keys, values, qs, query, place, olds, scores, top, acc, bases, starts, sems = refs
     x, z, c = place_of()
     copies = [
         pltpu.make_async_copy(kv_in[a], kv.at[pl.ds(N_X * a, N_X)], sems.at[N_X + a]) for a in range(arrays)
     ]
-    copies += [pltpu.make_async_copy(q_in[d], qs.at[d], sems.at[d]) for d in range(N_X)]
+    copies += [
+        pltpu.make_async_copy(q_in[d], qs.at[lax.rem(x - d + N_X, N_X)], sems.at[d]) for d in range(N_X)
+    ]
     for copy in copies:
         copy.start()
     for copy in copies:
@@ -210,132 +212,147 @@
         piece = lax.rem(c + tc, 2) * 16 + lax.rem(tz - z + N_Z, N_Z) * 4 + lax.rem(x - tx + N_X, N_X)
         count = jnp.max(kv[piece, META : META + 1, :HD].astype(f32)).astype(jnp.int32)
         starts[t] = n
+        at = pl.ds(pl.multiple_of(n * ROW, ROW), META)
+        keys[at, :] = kv[piece, :META, :HD]
+        values[at, :] = kv[piece, :META, HD:]
         for j in range(KEEP):
-            codes[n + j] = piece * KEEP + j
             bases[n + j] = t * PLEN
         n = n + count
     starts[N_SEQ] = n
+    values[pl.ds(pl.multiple_of(n * ROW, ROW), 2 * STEP * ROW), :] = jnp.zeros((2 * STEP * ROW, HD), bf16)
     for j in range(2 * STEP):
-        codes[n + j] = 0
         bases[n + j] = FAR * PLEN
 
     lane = lax.broadcasted_iota(jnp.int32, (1, 2 * ROW), 1)
     w = GQ * HD
 
-    def block(code, cols):
-        piece = code // KEEP
-        first = pl.multiple_of(lax.rem(code, KEEP) * ROW, ROW)
-        return kv[piece, pl.ds(first, ROW), cols]
-
-    def gather(g, count, cols):
-        return jnp.concatenate([block(codes[g * STEP + u], cols) for u in range(count * STEP)], axis=0)
-
-    def visit(d, carry):
-        shard = seq_of(lax.rem(x - d + N_X, N_X), z, c)
-        q = jnp.concatenate([qs[d, :, g * HD : (g + 1) * HD] for g in range(GQ)], axis=0)
-        begin = starts[shard]
-        end = starts[shard + 1]
-        for j in range(KEEP):
-
-            @pl.when(begin + j < end)
-            def _():
-                number = jnp.max(kv[d, META + 1 + j : META + 2 + j, :HD].astype(f32)).astype(jnp.int32)
-                bases[begin + j] = shard * PLEN + number * BLK + half * ROW
+    def gather(ref, g):
+        return ref[pl.ds(pl.multiple_of(g * STEP * ROW, STEP * ROW), STEP * ROW), :]
+
+    def columns(pair, first, width):
+        parts = [qs[2 * pair + r, :, first : first + width] for r in range(2)]
+        return jnp.concatenate([parts[r] for r in range(2) for _ in range(GQ)], axis=0)
+
+    def visit(pair, carry):
+        shards = [seq_of(2 * pair + r, z, c) for r in range(2)]
+        begins = [starts[shards[r]] for r in range(2)]
+        ends = [starts[shards[r] + 1] for r in range(2)]
+        for r in range(2):
+            piece = lax.rem(x - (2 * pair + r) + N_X, N_X)
+            for j in range(KEEP):
+
+                @pl.when(begins[r] + j < ends[r])
+                def _():
+                    number = jnp.max(kv[piece, META + 1 + j : META + 2 + j, :HD].astype(f32)).astype(jnp.int32)
+                    bases[begins[r] + j] = shards[r] * PLEN + number * BLK + half * ROW
+
+            for g in range(GQ):
+                rows = slice((r * GQ + g) * R_DEV, (r * GQ + g + 1) * R_DEV)
+                query[rows, :] = qs[2 * pair + r, :, g * HD : (g + 1) * HD]
+        high = columns(pair, w + 2 * HD, HD).astype(f32)
+        low = columns(pair, w + 3 * HD, HD).astype(f32)
+        row = lax.broadcasted_iota(jnp.int32, (2 * ROWS, 1), 0)
+        first = jnp.where(row < ROWS, shards[0] * PLEN, shards[1] * PLEN).astype(f32)
+        place[...] = high * 16 + low + first
 
         if half:
-            old = jnp.broadcast_to(state_in[d, :, 0:1], (ROWS, HD))
+            state = jnp.concatenate([stats[2 * pair + r] for r in range(2)], axis=0)
+            old = jnp.broadcast_to(state[:, 0:1], (2 * ROWS, HD))
+            olds[...] = old
         else:
-            own_k = jnp.concatenate([qs[d, :, w : w + HD]] * GQ, axis=0).astype(f32)
-            own = jnp.sum(q.astype(f32) * own_k, axis=1, keepdims=True) * EXP_SCALE
-            old = jnp.broadcast_to(own, (ROWS, HD))
+            own_k = columns(pair, w, HD).astype(f32)
+            own = jnp.sum(query[...].astype(f32) * own_k, axis=1, keepdims=True) * EXP_SCALE
+            old = jnp.broadcast_to(own, (2 * ROWS, HD))
+            olds[...] = old
         top[...] = old
 
-        def first_pass(g, count, masked):
-            s = lax.dot_general(q, gather(g, count, slice(0, HD)), NT, preferred_element_type=f32)
-            best = top[...]
-            for u in range(count * STEP // 2):
+        def first_pass(g, rows, masked):
+            s = lax.dot_general(query[rows, :], gather(keys, g), NT, preferred_element_type=f32)
+            best = top[rows, :]
+            for u in range(STEP // 2):
                 part = s[:, u * HD : (u + 1) * HD] * EXP_SCALE
                 if masked:
                     b0 = bases[g * STEP + 2 * u]
                     b1 = bases[g * STEP + 2 * u + 1] - ROW
                     spot = (jnp.where(lane < ROW, b0, b1) + lane).astype(f32)
-                    high = qs[d, :, w + 2 * HD : w + 3 * HD].astype(f32)
-                    place = high * 16 + qs[d, :, w + 3 * HD :].astype(f32)
-                    spot = spot - (shard * PLEN).astype(f32)
-                    part = jnp.concatenate(
-                        [
-                            jnp.where(spot < place, part[r * R_DEV : (r + 1) * R_DEV], -jnp.inf)
-                            for r in range(GQ)
-                        ],
-                        axis=0,
-                    )
-                half_step = STEP // 2
-                at = slice((u % half_step) * HD, (u % half_step + 1) * HD)
-                scores[g + u // half_step, :, at] = part
+                    part = jnp.where(spot < place[rows, :], part, -jnp.inf)
+                scores[g, rows, u * HD : (u + 1) * HD] = part
                 best = jnp.maximum(best, part)
-            top[...] = best
-
-        pairs = begin // (2 * STEP)
-        groups = (end + STEP - 1) // STEP
-
-        @pl.loop(0, pairs)
-        def _(i):
-            first_pass(2 * i, 2, False)
-
-        @pl.loop(2 * pairs, groups)
+            top[rows, :] = best
+
+        everything, upper = slice(0, 2 * ROWS), slice(ROWS, 2 * ROWS)
+        plain = begins[0] // STEP
+        both = (ends[0] + STEP - 1) // STEP
+        most = (ends[1] + STEP - 1) // STEP
+
+        @pl.loop(0, plain)
         def _(g):
-            first_pass(g, 1, True)
+            first_pass(g, everything, False)
+
+        @pl.loop(plain, both)
+        def _(g):
+            first_pass(g, everything, True)
+
+        @pl.loop(both, most)
+        def _(g):
+            first_pass(g, upper, True)
 
         m = jnp.max(top[...], axis=1, keepdims=True)
-        wide = jnp.broadcast_to(m, (ROWS, HD))
+        wide = jnp.broadcast_to(m, (2 * ROWS, HD))
         top[...] = wide
         if half:
-            alpha = jnp.exp2(old - wide)
-            acc[:, :HD] = acc_in[d] * alpha
-            acc[:, HD:] = jnp.where(lane == 0, alpha * jnp.broadcast_to(state_in[d, :, ROW : ROW + 1], (ROWS, HD)), 0.0)
+            alpha = jnp.exp2(olds[...] - wide)
+            mixed = jnp.concatenate([mixes[2 * pair + r] for r in range(2)], axis=0)
+            state = jnp.concatenate([stats[2 * pair + r] for r in range(2)], axis=0)
+            acc[:, :HD] = mixed * alpha
+            acc[:, HD:] = jnp.where(
+                lane == 0, alpha * jnp.broadcast_to(state[:, ROW : ROW + 1], (2 * ROWS, HD)), 0.0
+            )
         else:
-            alpha = jnp.exp2(old - wide).astype(bf16).astype(f32)
-            own_v = jnp.concatenate([qs[d, :, w + HD : w + 2 * HD]] * GQ, axis=0).astype(f32)
-            acc[:, :HD] = alpha * own_v
+            alpha = jnp.exp2(olds[...] - wide).astype(bf16).astype(f32)
+            acc[:, :HD] = alpha * columns(pair, w + HD, HD).astype(f32)
             acc[:, HD:] = jnp.where(lane == 0, alpha, 0.0)
 
-        def second_pass(g, count):
+        def second_pass(g, rows):
             ps = []
-            total = acc[:, HD:]
-            for u in range(count * STEP // 2):
-                half_step = STEP // 2
-                at = slice((u % half_step) * HD, (u % half_step + 1) * HD)
-                p = jnp.exp2(scores[g + u // half_step, :, at] - top[...]).astype(bf16)
-                total = total + p.astype(f32)
-                ps.append(p)
-            acc[:, HD:] = total
+            total = acc[rows, HD:]
+            for u in range(STEP // 2):
+                p = jnp.exp2(scores[g, rows, u * HD : (u + 1) * HD] - top[rows, :])
+                total = total + p
+                ps.append(p.astype(bf16))
+            acc[rows, HD:] = total
             p = jnp.concatenate(ps, axis=1)
-            acc[:, :HD] += jnp.dot(p, gather(g, count, slice(HD, KV2)), preferred_element_type=f32)
-
-        @pl.loop(0, groups // 2)
-        def _(i):
-            second_pass(2 * i, 2)
-
-        @pl.when(groups % 2 == 1)
-        def _():
-            second_pass(groups - 1, 1)
+            acc[rows, :HD] += jnp.dot(p, gather(values, g), preferred_element_type=f32)
+
+        @pl.loop(0, both)
+        def _(g):
+            second_pass(g, everything)
+
+        @pl.loop(both, most)
+        def _(g):
+            second_pass(g, upper)
 
         total = jnp.sum(acc[:, HD:], axis=1, keepdims=True)
         if half:
             out = (acc[:, :HD] / total).astype(bf16)
-            for e in range(N_X):
-
-                @pl.when(d == e)
-                def _():
-                    for g in range(GQ):
-                        outs[e][:, g * HD : (g + 1) * HD] = out[g * R_DEV : (g + 1) * R_DEV]
+            for r in range(2):
+                d = lax.rem(x - (2 * pair + r) + N_X, N_X)
+                for e in range(N_X):
+
+                    @pl.when(d == e)
+                    def _():
+                        for g in range(GQ):
+                            rows = slice((r * GQ + g) * R_DEV, (r * GQ + g + 1) * R_DEV)
+                            outs[e][:, g * HD : (g + 1) * HD] = out[rows]
 
         else:
-            acc_out[d] = acc[:, :HD]
-            state_out[d] = jnp.where(lane < ROW, top[...], total)
+            for r in range(2):
+                rows = slice(r * ROWS, (r + 1) * ROWS)
+                mixes[2 * pair + r] = acc[rows, :HD]
+                stats[2 * pair + r] = jnp.where(lane < ROW, top[rows, :], total[rows])
         return carry
 
-    lax.fori_loop(0, N_X, visit, 0)
+    lax.fori_loop(0, N_X // 2, visit, 0)
 
 
 def read(half, kv_arrays, q_arrays, state):
@@ -352,16 +369,20 @@
         out_specs=(vmem,) * (N_X if half else 2),
         scratch_shapes=[
             pltpu.VMEM((PIECES, PIECE, KV2), bf16),
+            pltpu.VMEM(((most + 2 * STEP) * ROW, HD), bf16),
+            pltpu.VMEM(((most + 2 * STEP) * ROW, HD), bf16),
             pltpu.VMEM((N_X, R_DEV, QW), bf16),
-            pltpu.VMEM((most // STEP, ROWS, STEP * ROW), f32),
-            pltpu.VMEM((ROWS, HD), f32),
-            pltpu.VMEM((ROWS, KV2), f32),
-            pltpu.SMEM((most + 2 * STEP,), jnp.int32),
+            pltpu.VMEM((2 * ROWS, HD), bf16),
+            pltpu.VMEM((2 * ROWS, HD), f32),
+            pltpu.VMEM((2 * ROWS, HD), f32),
+            pltpu.VMEM((most // STEP, 2 * ROWS, STEP * ROW), f32),
+            pltpu.VMEM((2 * ROWS, HD), f32),
+            pltpu.VMEM((2 * ROWS, KV2), f32),
             pltpu.SMEM((most + 2 * STEP,), jnp.int32),
             pltpu.SMEM((N_SEQ + 1,), jnp.int32),
             pltpu.SemaphoreType.DMA((N_X + arrays,)),
         ],
-        compiler_params=pltpu.CompilerParams(vmem_limit_bytes=40 << 20),
+        compiler_params=pltpu.CompilerParams(vmem_limit_bytes=44 << 20),
         cost_estimate=pl.CostEstimate(flops=5 << 30, bytes_accessed=8 << 20, transcendentals=6 << 20),
     )(*kv_arrays, *q_arrays, *state)
 
@@ -412,12 +433,16 @@
     passage_out = encode(passage_q, passage_k, passage_v, 0, 2, None)
     rel, passage_out, q_arrays = fence((rel, passage_out, q_arrays))
 
-    mine0 = around_z(across_x(choose(rel, first, near0)))
+    here0 = across_x(choose(rel, first, near0))
+    passage_out = encode(passage_q, passage_k, passage_v, 2, 1, passage_out)
+    here0, passage_out = fence((here0, passage_out))
+    mine0 = around_z(here0)
     other0 = [swap(mine0[0])]
-    rel, passage_out, other0 = fence((rel, passage_out, other0))
-    passage_out = encode(passage_q, passage_k, passage_v, 2, 2, passage_out)
-    rel, passage_out = fence((rel, passage_out))
-    mine1 = around_z(across_x(choose(rel, second, near1)))
+    rel, other0 = fence((rel, other0))
+    here1 = across_x(choose(rel, second, near1))
+    passage_out = encode(passage_q, passage_k, passage_v, 3, 1, passage_out)
+    here1, passage_out = fence((here1, passage_out))
+    mine1 = around_z(here1)
     kv0 = mine0 + other0 + [swap(t) for t in mine0[1:]]
     state = read(0, kv0, q_arrays, ())
     other1 = [swap(mine1[0])]

time: 140 us -> 141 us (level)
  local copies, waits for them, and re-layouts: 0.1 us -> 4.51 us
  starting transfers between devices: 37.7 us -> 34.1 us
    unnamed x6 -> x26, local copies, waits for them, and re-layouts: 0.01 us -> 3.74 us
    ppermute x26, starting transfers between devices: 31.9 us -> 28.3 us  [shift_seq(): return lax.ppermute(a, 'seq', seq_pairs(dx, dz, dc))]
    pallas_call x2 -> x3, Pallas kernels: 12.9 us -> 15.2 us  [encode(): pl.pallas_call(kernel, out_shape=jax.ShapeDtypeStruct((PLEN, HQ * HD), bf...]
    pallas_call x2, Pallas kernels: 30 us -> 28.4 us  [read(): pl.pallas_call(functools.partial(reader_kernel, half), out_shape=(out,) *...]
  transfers between devices with their start and end apart: 32 -> 32, of which waited for: 19 -> 14; matrix products, arithmetic and copies ran while one was open for 1% -> 2% of each run, Pallas kernels for 23% -> 24%
where the time goes in v1:
time: 141 us
  Pallas kernels  49.8 us (35%)
  waiting for transfers between devices  47.3 us (34%)
  starting transfers between devices  34.1 us (24%)
  local copies, waits for them, and re-layouts  4.51 us (3%)
  other arithmetic  3.37 us (2%)
  between operations  1.61 us (1%)
    ppermute x26, waiting for transfers between devices, shift_seq(): return lax.ppermute(a, 'seq', seq_pairs(dx, dz, dc))  41.1 us
    pallas_call x2, Pallas kernels, read(): pl.pallas_call(functools.partial(reader_kernel, half), out_shape=(out,) *...  28.4 us
    ppermute x26, starting transfers between devices, shift_seq(): return lax.ppermute(a, 'seq', seq_pairs(dx, dz, dc))  28.3 us
    pallas_call x3, Pallas kernels, encode(): pl.pallas_call(kernel, out_shape=jax.ShapeDtypeStruct((PLEN, HQ * HD), bf...  15.2 us
    ppermute x6, waiting for transfers between devices, shift_y(): return lax.ppermute(a, 'grp', [(i, (i + k) % N_GRP) for i in range(N_GRP)])  6.14 us
    ppermute x6, starting transfers between devices, shift_y(): return lax.ppermute(a, 'grp', [(i, (i + k) % N_GRP) for i in range(N_GRP)])  5.82 us
    pallas_call x2, Pallas kernels, pack(): pl.pallas_call(functools.partial(pack_kernel, half), out_shape=jax.ShapeD...  4.13 us
    unnamed x26, local copies, waits for them, and re-layouts  3.74 us
  transfers between devices with their start and end apart: 32, of which 14 were waited for; matrix products, arithmetic and copies ran while one was open for 2% of the time, Pallas kernels for 24%

profile of v1, /device:TPU:1, one launch (start us, length us, event | category | flops | bytes accessed | tf_op | source)
XLA Modules:
  0.0 140.7 jit_solution(2613248014301053502)
XLA Ops:
  0.6 2.1 %shard_map.105 = bf16[4,208,256]{2,1,0:T(8,128)(2,1)} custom-call(s32[1,4]{1,0:T(1,128)} %kept_ref.3, bf16[512,512]{1,0:T(8,128)(2,1)} %k_ref.9, bf16[512,512]{1,0:T(8,128)(2,1)} %v_ref.9), custom_call_target="tpu_custom_call" | custom-call | tf_op jit(solution)/shard_map/pallas_call | solution.py:95
  2.7 3.6 %collective-permute-start.3 = (bf16[4,208,256]{2,1,0:T(8,128)(2,1)}, bf16[4,208,256]{2,1,0:T(8,128)(2,1)S(1)}, u32[]{:S(2)}, u32[]{:S(2)}) collective-permute-start(bf16[4,208,256]{2,1,0:T(8,128)(2,1)} %shard_map.105), channel_id=1, source_target_pairs={{0,96},{32,0},{64,32},{96,64},{1,97},{33,1},{65,33},{97,65},{2,98}... | collective-permute-start | bytes 1277960 | tf_op jit(solution)/shard_map/ppermute | solution.py:47
  7.3 2.1 %queries.1 = (bf16[64,1536]{1,0:T(8,128)(2,1)}, bf16[64,1536]{1,0:T(8,128)(2,1)}, bf16[64,1536]{1,0:T(8,128)(2,1)}, bf16[64,1536]{1,0:T(8,128)(2,1)}) custom-call(s32[1,64]{1,0:T(1,128)} %pos_ref.1, bf16[64,4096]{1,0:T(8,128)(2,1)} %bitcast.10, bf16[64,512]{1,0:T(8,128)(2,1)} %bitcast.11, bf16[64,512]{1,0:T(8,128)(2,1)} %bitcast.12), custom_call_target="tpu_custom_call" | custom-call | tf_op jit(solution)/shard_map/queries/pallas_call | solution.py:125
  9.4 1.2 collective-permute-start
  10.6 2.5 %collective-permute-start.1 = (bf16[64,1536]{1,0:T(8,128)(2,1)}, bf16[64,1536]{1,0:T(8,128)(2,1)S(1)}, u32[]{:S(2)}, u32[]{:S(2)}) collective-permute-start(bf16[64,1536]{1,0:T(8,128)(2,1)} %get-tuple-element.32), channel_id=1, source_target_pairs={{0,16},{1,17},{2,18},{3,19},{4,20},{5,21},{6,22},{7,23},{8,24},{9,... | collective-permute-start | bytes 589832 | tf_op jit(solution)/shard_map/ppermute | solution.py:60
  13.8 1.9 %collective-permute-done.refs_9_ = bf16[64,1536]{1,0:T(8,128)(2,1)S(1)} collective-permute-done((bf16[64,1536]{1,0:T(8,128)(2,1)}, bf16[64,1536]{1,0:T(8,128)(2,1)S(1)}, u32[]{:S(2)}, u32[]{:S(2)}) %collective-permute-start) | collective-permute-done | bytes 196640 | tf_op jit(solution)/shard_map/ppermute | solution.py:60
  15.7 1.3 collective-permute-start.2
  17.0 6.5 %shard_map.104.rest_0_ = bf16[512,4096]{1,0:T(8,128)(2,1)} custom-call(bf16[512,4096]{1,0:T(8,128)(2,1)} %q_ref.5, bf16[512,512]{1,0:T(8,128)(2,1)} %k_ref.9, bf16[512,512]{1,0:T(8,128)(2,1)} %v_ref.9), custom_call_target="tpu_custom_call" | custom-call | flops 2147483648 | bytes 4718592 | tf_op jit(solution)/shard_map/pallas_call | solution.py:171
  24.1 4.8 %collective-permute-done.5 = bf16[4,208,256]{2,1,0:T(8,128)(2,1)S(1)} collective-permute-done((bf16[4,208,256]{2,1,0:T(8,128)(2,1)}, bf16[4,208,256]{2,1,0:T(8,128)(2,1)S(1)}, u32[]{:S(2)}, u32[]{:S(2)}) %collective-permute-start.5) | collective-permute-done | bytes 426016 | tf_op jit(solution)/shard_map/ppermute | solution.py:47
  29.0 1.3 collective-permute-start.6
  30.2 2.5 %collective-permute-start.7 = (bf16[1,208,256]{2,1,0:T(8,128)(2,1)S(1)}, bf16[1,208,256]{2,1,0:T(8,128)(2,1)S(1)}, u32[]{:S(2)}, u32[]{:S(2)}) collective-permute-start(bf16[1,208,256]{2,1,0:T(8,128)(2,1)S(1)} %get-tuple-element.68), channel_id=1, source_target_pairs={{0,16},{1,17},{2,18},{3,19},{4,20},{5,21},{6,22},{7,23},{8,24},{9,... | collective-permute-start | bytes 319496 | tf_op jit(solution)/shard_map/ppermute | solution.py:60
  32.7 1.2 collective-permute-start.8
  33.8 2.1 %shard_map.107 = bf16[4,208,256]{2,1,0:T(8,128)(2,1)} custom-call(s32[1,4]{1,0:T(1,128)} %kept_ref.3, bf16[512,512]{1,0:T(8,128)(2,1)} %k_ref.9, bf16[512,512]{1,0:T(8,128)(2,1)} %v_ref.9), custom_call_target="tpu_custom_call" | custom-call | tf_op jit(solution)/shard_map/pallas_call | solution.py:95
  35.9 4.4 %shard_map.106.rest_0_ = bf16[512,4096]{1,0:T(8,128)(2,1)} custom-call(bf16[512,4096]{1,0:T(8,128)(2,1)} %q_ref.5, bf16[512,512]{1,0:T(8,128)(2,1)} %k_ref.9, bf16[512,512]{1,0:T(8,128)(2,1)} %v_ref.9, bf16[512,4096]{1,0:T(8,128)(2,1)} %shard_map.104.rest_0_), custom_call_target="tpu_custom_call", output_to_operand_aliasing={{}: (3, {})} | custom-call | flops 1073741824 | bytes 2359296 | tf_op jit(solution)/shard_map/pallas_call | solution.py:171
  40.4 2.0 %collective-permute-start.9 = (bf16[4,208,256]{2,1,0:T(8,128)(2,1)S(1)}, bf16[4,208,256]{2,1,0:T(8,128)(2,1)S(1)}, u32[]{:S(2)}, u32[]{:S(2)}) collective-permute-start(bf16[4,208,256]{2,1,0:T(8,128)(2,1)S(1)} %pad_maximum_fusion.refs_0_), channel_id=1, source_target_pairs={{0,1},{1,0},{2,3},{3,2},{4,5},{5,4},{6,7},{7,6},{8,9},{9,8},{10,11... | collective-permute-start | bytes 1277960 | tf_op jit(solution)/shard_map/ppermute | solution.py:60
  42.4 3.8 %collective-permute-start.16 = (bf16[4,208,256]{2,1,0:T(8,128)(2,1)S(1)}, bf16[4,208,256]{2,1,0:T(8,128)(2,1)S(1)}, u32[]{:S(2)}, u32[]{:S(2)}) collective-permute-start(bf16[4,208,256]{2,1,0:T(8,128)(2,1)S(1)} %pad_maximum_fusion.refs_0_), channel_id=1, source_target_pairs={{0,6},{1,7},{2,0},{3,1},{4,2},{5,3},{6,4},{7,5},{8,14},{9,15},{10,... | collective-permute-start | bytes 1277960 | tf_op jit(solution)/shard_map/ppermute | solution.py:60
  48.1 16.3 %collective-permute-done.16.refs_1_ = bf16[4,208,256]{2,1,0:T(8,128)(2,1)S(1)} collective-permute-done((bf16[4,208,256]{2,1,0:T(8,128)(2,1)S(1)}, bf16[4,208,256]{2,1,0:T(8,128)(2,1)S(1)}, u32[]{:S(2)}, u32[]{:S(2)}) %collective-permute-start.16) | collective-permute-done | bytes 426016 | tf_op jit(solution)/shard_map/ppermute | solution.py:60
  65.3 2.7 %collective-permute-done.18.refs_3_ = bf16[4,208,256]{2,1,0:T(8,128)(2,1)S(1)} collective-permute-done((bf16[4,208,256]{2,1,0:T(8,128)(2,1)S(1)}, bf16[4,208,256]{2,1,0:T(8,128)(2,1)S(1)}, u32[]{:S(2)}, u32[]{:S(2)}) %collective-permute-start.18) | collective-permute-done | bytes 426016 | tf_op jit(solution)/shard_map/ppermute | solution.py:60
  69.5 1.2 select_select_fusion
  72.3 7.0 %collective-permute-done.13 = bf16[1,208,256]{2,1,0:T(8,128)(2,1)} collective-permute-done((bf16[1,208,256]{2,1,0:T(8,128)(2,1)S(1)}, bf16[1,208,256]{2,1,0:T(8,128)(2,1)}, u32[]{:S(2)}, u32[]{:S(2)}) %collective-permute-start.13) | collective-permute-done | bytes 106528 | tf_op jit(solution)/shard_map/ppermute | solution.py:60
  79.3 4.4 %shard_map.108 = bf16[512,4096]{1,0:T(8,128)(2,1)} custom-call(bf16[512,4096]{1,0:T(8,128)(2,1)} %q_ref.5, bf16[512,512]{1,0:T(8,128)(2,1)} %k_ref.9, bf16[512,512]{1,0:T(8,128)(2,1)} %v_ref.9, bf16[512,4096]{1,0:T(8,128)(2,1)} %shard_map.106.rest_0_), custom_call_target="tpu_custom_call", output_to_operand_aliasing={{}: (3, {})} | custom-call | flops 1073741824 | bytes 2359296 | tf_op jit(solution)/shard_map/pallas_call | solution.py:171
  83.7 1.1 pad_maximum_fusion.1.refs_0_
  84.8 1.9 %collective-permute-start.22 = (bf16[4,208,256]{2,1,0:T(8,128)(2,1)S(1)}, bf16[4,208,256]{2,1,0:T(8,128)(2,1)S(1)}, u32[]{:S(2)}, u32[]{:S(2)}) collective-permute-start(bf16[4,208,256]{2,1,0:T(8,128)(2,1)S(1)} %pad_maximum_fusion.1.refs_0_), channel_id=1, source_target_pairs={{0,1},{1,0},{2,3},{3,2},{4,5},{5,4},{6,7},{7,6},{8,9},{9,8},{10,11... | collective-permute-start | bytes 1277960 | tf_op jit(solution)/shard_map/ppermute | solution.py:60
  86.7 2.9 %collective-permute-start.23 = (bf16[4,208,256]{2,1,0:T(8,128)(2,1)S(1)}, bf16[4,208,256]{2,1,0:T(8,128)(2,1)S(1)}, u32[]{:S(2)}, u32[]{:S(2)}) collective-permute-start(bf16[4,208,256]{2,1,0:T(8,128)(2,1)S(1)} %pad_maximum_fusion.1.refs_0_), channel_id=1, source_target_pairs={{0,6},{1,7},{2,0},{3,1},{4,2},{5,3},{6,4},{7,5},{8,14},{9,15},{10,... | collective-permute-start | bytes 1277960 | tf_op jit(solution)/shard_map/ppermute | solution.py:60
  94.2 13.9 %shard_map.109 = (f32[4,512,128]{2,1,0:T(8,128)S(1)}, f32[4,512,128]{2,1,0:T(8,128)S(1)}) custom-call(bf16[4,208,256]{2,1,0:T(8,128)(2,1)S(1)} %pad_maximum_fusion.refs_0_, bf16[4,208,256]{2,1,0:T(8,128)(2,1)S(1)} %collective-permute-done.16.refs_1_, bf16[4,208,256]{2,1,0:T(8,128)(2,1)S(1)} %collective-permute-done.17.refs_2_, ...), custom_call_target="tpu_custom_call" | custom-call | flops 5368709120 | bytes 8388608 | tf_op jit(solution)/shard_map/pallas_call | solution.py:365
  108.1 3.9 %collective-permute-done.25.refs_3_ = bf16[4,208,256]{2,1,0:T(8,128)(2,1)S(1)} collective-permute-done((bf16[4,208,256]{2,1,0:T(8,128)(2,1)S(1)}, bf16[4,208,256]{2,1,0:T(8,128)(2,1)S(1)}, u32[]{:S(2)}, u32[]{:S(2)}) %collective-permute-start.25) | collective-permute-done | bytes 426016 | tf_op jit(solution)/shard_map/ppermute | solution.py:60
  115.2 14.5 %shard_map.110 = (bf16[64,1024]{1,0:T(8,128)(2,1)S(1)}, bf16[64,1024]{1,0:T(8,128)(2,1)S(1)}, bf16[64,1024]{1,0:T(8,128)(2,1)S(1)}, bf16[64,1024]{1,0:T(8,128)(2,1)S(1)}) custom-call(bf16[4,208,256]{2,1,0:T(8,128)(2,1)S(1)} %pad_maximum_fusion.1.refs_0_, bf16[4,208,256]{2,1,0:T(8,128)(2,1)S(1)} %collective-permute-done.23.refs_1_, ...), custom_call_target="tpu_custom_call" | custom-call | flops 5368709120 | bytes 8388608 | tf_op jit(solution)/shard_map/pallas_call | solution.py:365
  129.7 1.0 collective-permute-start.29
  130.7 2.0 %collective-permute-start.30 = (bf16[64,1024]{1,0:T(8,128)(2,1)S(1)}, bf16[64,1024]{1,0:T(8,128)(2,1)S(1)}, u32[]{:S(2)}, u32[]{:S(2)}) collective-permute-start(bf16[64,1024]{1,0:T(8,128)(2,1)S(1)} %get-tuple-element.56), channel_id=1, source_target_pairs={{0,16},{1,17},{2,18},{3,19},{4,20},{5,21},{6,22},{7,23},{8,24},{9,... | collective-permute-start | bytes 393224 | tf_op jit(solution)/shard_map/ppermute | solution.py:60
  132.6 1.5 %collective-permute-done.29 = bf16[64,1024]{1,0:T(8,128)(2,1)S(1)} collective-permute-done((bf16[64,1024]{1,0:T(8,128)(2,1)S(1)}, bf16[64,1024]{1,0:T(8,128)(2,1)S(1)}, u32[]{:S(2)}, u32[]{:S(2)}) %collective-permute-start.29) | collective-permute-done | bytes 131104 | tf_op jit(solution)/shard_map/ppermute | solution.py:60
  134.2 2.1 %collective-permute-done.30 = bf16[64,1024]{1,0:T(8,128)(2,1)S(1)} collective-permute-done((bf16[64,1024]{1,0:T(8,128)(2,1)S(1)}, bf16[64,1024]{1,0:T(8,128)(2,1)S(1)}, u32[]{:S(2)}, u32[]{:S(2)}) %collective-permute-start.30) | collective-permute-done | bytes 131104 | tf_op jit(solution)/shard_map/ppermute | solution.py:60
  136.3 3.5 %collective-permute-done.31 = bf16[64,1024]{1,0:T(8,128)(2,1)S(1)} collective-permute-done((bf16[64,1024]{1,0:T(8,128)(2,1)S(1)}, bf16[64,1024]{1,0:T(8,128)(2,1)S(1)}, u32[]{:S(2)}, u32[]{:S(2)}) %collective-permute-start.31) | collective-permute-done | bytes 131104 | tf_op jit(solution)/shard_map/ppermute | solution.py:60
  (74 shorter events, 16.2 us)
Async XLA Ops:
  2.7 21.4 %collective-permute-start.3 = (bf16[4,208,256]{2,1,0:T(8,128)(2,1)}, bf16[4,208,256]{2,1,0:T(8,128)(2,1)S(1)}, u32[]{:S(2)}, u32[]{:S(2)}) collective-permute-start(bf16[4,208,256]{2,1,0:T(8,128)(2,1)} %shard_map.105), channel_id=1, source_target_pairs={{0,96},{32,0},{64,32},{96,64},{1,97},{33,1},{65,33},{97,65},{2,98}... | collective-permute-start | bytes 1277960 | tf_op jit(solution)/shard_map/ppermute | solution.py:47
  6.2 17.8 %collective-permute-start.4 = (bf16[4,208,256]{2,1,0:T(8,128)(2,1)}, bf16[4,208,256]{2,1,0:T(8,128)(2,1)S(1)}, u32[]{:S(2)}, u32[]{:S(2)}) collective-permute-start(bf16[4,208,256]{2,1,0:T(8,128)(2,1)} %shard_map.105), channel_id=1, source_target_pairs={{0,64},{32,96},{64,0},{96,32},{1,65},{33,97},{65,1},{97,33},{2,66}... | collective-permute-start | bytes 1277960 | tf_op jit(solution)/shard_map/ppermute | solution.py:47
  6.6 22.2 %collective-permute-start.5 = (bf16[4,208,256]{2,1,0:T(8,128)(2,1)}, bf16[4,208,256]{2,1,0:T(8,128)(2,1)S(1)}, u32[]{:S(2)}, u32[]{:S(2)}) collective-permute-start(bf16[4,208,256]{2,1,0:T(8,128)(2,1)} %shard_map.105), channel_id=1, source_target_pairs={{0,32},{32,64},{64,96},{96,0},{1,33},{33,65},{65,97},{97,1},{2,34}... | collective-permute-start | bytes 1277960 | tf_op jit(solution)/shard_map/ppermute | solution.py:47
  9.4 6.4 %collective-permute-start = (bf16[64,1536]{1,0:T(8,128)(2,1)}, bf16[64,1536]{1,0:T(8,128)(2,1)S(1)}, u32[]{:S(2)}, u32[]{:S(2)}) collective-permute-start(bf16[64,1536]{1,0:T(8,128)(2,1)} %get-tuple-element.31), channel_id=1, source_target_pairs={{0,8},{1,9},{2,10},{3,11},{4,12},{5,13},{6,14},{7,15},{8,16},{9,17... | collective-permute-start | bytes 589832 | tf_op jit(solution)/shard_map/ppermute | solution.py:60
  10.6 12.9 %collective-permute-start.1 = (bf16[64,1536]{1,0:T(8,128)(2,1)}, bf16[64,1536]{1,0:T(8,128)(2,1)S(1)}, u32[]{:S(2)}, u32[]{:S(2)}) collective-permute-start(bf16[64,1536]{1,0:T(8,128)(2,1)} %get-tuple-element.32), channel_id=1, source_target_pairs={{0,16},{1,17},{2,18},{3,19},{4,20},{5,21},{6,22},{7,23},{8,24},{9,... | collective-permute-start | bytes 589832 | tf_op jit(solution)/shard_map/ppermute | solution.py:60
  15.7 7.8 %collective-permute-start.2 = (bf16[64,1536]{1,0:T(8,128)(2,1)}, bf16[64,1536]{1,0:T(8,128)(2,1)S(1)}, u32[]{:S(2)}, u32[]{:S(2)}) collective-permute-start(bf16[64,1536]{1,0:T(8,128)(2,1)} %get-tuple-element.33), channel_id=1, source_target_pairs={{0,24},{1,25},{2,26},{3,27},{4,28},{5,29},{6,30},{7,31},{8,0},{9,1... | collective-permute-start | bytes 589832 | tf_op jit(solution)/shard_map/ppermute | solution.py:60
  29.0 11.3 %collective-permute-start.6 = (bf16[1,208,256]{2,1,0:T(8,128)(2,1)S(1)}, bf16[1,208,256]{2,1,0:T(8,128)(2,1)S(1)}, u32[]{:S(2)}, u32[]{:S(2)}) collective-permute-start(bf16[1,208,256]{2,1,0:T(8,128)(2,1)S(1)} %get-tuple-element.69), channel_id=1, source_target_pairs={{0,8},{1,9},{2,10},{3,11},{4,12},{5,13},{6,14},{7,15},{8,16},{9,17... | collective-permute-start | bytes 319496 | tf_op jit(solution)/shard_map/ppermute | solution.py:60
  30.2 10.0 %collective-permute-start.7 = (bf16[1,208,256]{2,1,0:T(8,128)(2,1)S(1)}, bf16[1,208,256]{2,1,0:T(8,128)(2,1)S(1)}, u32[]{:S(2)}, u32[]{:S(2)}) collective-permute-start(bf16[1,208,256]{2,1,0:T(8,128)(2,1)S(1)} %get-tuple-element.68), channel_id=1, source_target_pairs={{0,16},{1,17},{2,18},{3,19},{4,20},{5,21},{6,22},{7,23},{8,24},{9,... | collective-permute-start | bytes 319496 | tf_op jit(solution)/shard_map/ppermute | solution.py:60
  32.7 7.6 %collective-permute-start.8 = (bf16[1,208,256]{2,1,0:T(8,128)(2,1)S(1)}, bf16[1,208,256]{2,1,0:T(8,128)(2,1)S(1)}, u32[]{:S(2)}, u32[]{:S(2)}) collective-permute-start(bf16[1,208,256]{2,1,0:T(8,128)(2,1)S(1)} %get-tuple-element.67), channel_id=1, source_target_pairs={{0,24},{1,25},{2,26},{3,27},{4,28},{5,29},{6,30},{7,31},{8,0},{9,1... | collective-permute-start | bytes 319496 | tf_op jit(solution)/shard_map/ppermute | solution.py:60
  35.9 10.9 %collective-permute-start.10 = (bf16[4,208,256]{2,1,0:T(8,128)(2,1)}, bf16[4,208,256]{2,1,0:T(8,128)(2,1)S(1)}, u32[]{:S(2)}, u32[]{:S(2)}) collective-permute-start(bf16[4,208,256]{2,1,0:T(8,128)(2,1)} %shard_map.107), channel_id=1, source_target_pairs={{0,96},{32,0},{64,32},{96,64},{1,97},{33,1},{65,33},{97,65},{2,98}... | collective-permute-start | bytes 1277960 | tf_op jit(solution)/shard_map/ppermute | solution.py:47
  40.4 6.8 %collective-permute-start.9 = (bf16[4,208,256]{2,1,0:T(8,128)(2,1)S(1)}, bf16[4,208,256]{2,1,0:T(8,128)(2,1)S(1)}, u32[]{:S(2)}, u32[]{:S(2)}) collective-permute-start(bf16[4,208,256]{2,1,0:T(8,128)(2,1)S(1)} %pad_maximum_fusion.refs_0_), channel_id=1, source_target_pairs={{0,1},{1,0},{2,3},{3,2},{4,5},{5,4},{6,7},{7,6},{8,9},{9,8},{10,11... | collective-permute-start | bytes 1277960 | tf_op jit(solution)/shard_map/ppermute | solution.py:60
  42.4 22.0 %collective-permute-start.16 = (bf16[4,208,256]{2,1,0:T(8,128)(2,1)S(1)}, bf16[4,208,256]{2,1,0:T(8,128)(2,1)S(1)}, u32[]{:S(2)}, u32[]{:S(2)}) collective-permute-start(bf16[4,208,256]{2,1,0:T(8,128)(2,1)S(1)} %pad_maximum_fusion.refs_0_), channel_id=1, source_target_pairs={{0,6},{1,7},{2,0},{3,1},{4,2},{5,3},{6,4},{7,5},{8,14},{9,15},{10,... | collective-permute-start | bytes 1277960 | tf_op jit(solution)/shard_map/ppermute | solution.py:60
  46.1 19.2 %collective-permute-start.17 = (bf16[4,208,256]{2,1,0:T(8,128)(2,1)S(1)}, bf16[4,208,256]{2,1,0:T(8,128)(2,1)S(1)}, u32[]{:S(2)}, u32[]{:S(2)}) collective-permute-start(bf16[4,208,256]{2,1,0:T(8,128)(2,1)S(1)} %pad_maximum_fusion.refs_0_), channel_id=1, source_target_pairs={{0,4},{1,5},{2,6},{3,7},{4,0},{5,1},{6,2},{7,3},{8,12},{9,13},{10,... | collective-permute-start | bytes 1277960 | tf_op jit(solution)/shard_map/ppermute | solution.py:60
  46.1 21.9 %collective-permute-start.18 = (bf16[4,208,256]{2,1,0:T(8,128)(2,1)S(1)}, bf16[4,208,256]{2,1,0:T(8,128)(2,1)S(1)}, u32[]{:S(2)}, u32[]{:S(2)}) collective-permute-start(bf16[4,208,256]{2,1,0:T(8,128)(2,1)S(1)} %pad_maximum_fusion.refs_0_), channel_id=1, source_target_pairs={{0,2},{1,3},{2,4},{3,5},{4,6},{5,7},{6,0},{7,1},{8,10},{9,11},{10,... | collective-permute-start | bytes 1277960 | tf_op jit(solution)/shard_map/ppermute | solution.py:60
  46.9 21.9 %collective-permute-start.11 = (bf16[4,208,256]{2,1,0:T(8,128)(2,1)}, bf16[4,208,256]{2,1,0:T(8,128)(2,1)}, u32[]{:S(2)}, u32[]{:S(2)}) collective-permute-start(bf16[4,208,256]{2,1,0:T(8,128)(2,1)} %shard_map.107), channel_id=1, source_target_pairs={{0,64},{32,96},{64,0},{96,32},{1,65},{33,97},{65,1},{97,33},{2,66}... | collective-permute-start | bytes 1277960 | tf_op jit(solution)/shard_map/ppermute | solution.py:47
  47.2 22.3 %collective-permute-start.12 = (bf16[4,208,256]{2,1,0:T(8,128)(2,1)}, bf16[4,208,256]{2,1,0:T(8,128)(2,1)}, u32[]{:S(2)}, u32[]{:S(2)}) collective-permute-start(bf16[4,208,256]{2,1,0:T(8,128)(2,1)} %shard_map.107), channel_id=1, source_target_pairs={{0,32},{32,64},{64,96},{96,0},{1,33},{33,65},{65,97},{97,1},{2,34}... | collective-permute-start | bytes 1277960 | tf_op jit(solution)/shard_map/ppermute | solution.py:47
  64.4 25.3 %collective-permute-start.19 = (bf16[4,208,256]{2,1,0:T(8,128)(2,1)S(1)}, bf16[4,208,256]{2,1,0:T(8,128)(2,1)S(1)}, u32[]{:S(2)}, u32[]{:S(2)}) collective-permute-start(bf16[4,208,256]{2,1,0:T(8,128)(2,1)S(1)} %collective-permute-done.16.refs_1_), channel_id=1, source_target_pairs={{0,1},{1,0},{2,3},{3,2},{4,5},{5,4},{6,7},{7,6},{8,9},{9,8},{10,11... | collective-permute-start | bytes 1277960 | tf_op jit(solution)/shard_map/ppermute | solution.py:60
  65.3 25.0 %collective-permute-start.20 = (bf16[4,208,256]{2,1,0:T(8,128)(2,1)S(1)}, bf16[4,208,256]{2,1,0:T(8,128)(2,1)S(1)}, u32[]{:S(2)}, u32[]{:S(2)}) collective-permute-start(bf16[4,208,256]{2,1,0:T(8,128)(2,1)S(1)} %collective-permute-done.17.refs_2_), channel_id=1, source_target_pairs={{0,1},{1,0},{2,3},{3,2},{4,5},{5,4},{6,7},{7,6},{8,9},{9,8},{10,11... | collective-permute-start | bytes 1277960 | tf_op jit(solution)/shard_map/ppermute | solution.py:60
  68.0 22.4 %collective-permute-start.21 = (bf16[4,208,256]{2,1,0:T(8,128)(2,1)S(1)}, bf16[4,208,256]{2,1,0:T(8,128)(2,1)S(1)}, u32[]{:S(2)}, u32[]{:S(2)}) collective-permute-start(bf16[4,208,256]{2,1,0:T(8,128)(2,1)S(1)} %collective-permute-done.18.refs_3_), channel_id=1, source_target_pairs={{0,1},{1,0},{2,3},{3,2},{4,5},{5,4},{6,7},{7,6},{8,9},{9,8},{10,11... | collective-permute-start | bytes 1277960 | tf_op jit(solution)/shard_map/ppermute | solution.py:60
  71.5 7.8 %collective-permute-start.13 = (bf16[1,208,256]{2,1,0:T(8,128)(2,1)S(1)}, bf16[1,208,256]{2,1,0:T(8,128)(2,1)}, u32[]{:S(2)}, u32[]{:S(2)}) collective-permute-start(bf16[1,208,256]{2,1,0:T(8,128)(2,1)S(1)} %get-tuple-element.65), channel_id=1, source_target_pairs={{0,8},{1,9},{2,10},{3,11},{4,12},{5,13},{6,14},{7,15},{8,16},{9,17... | collective-permute-start | bytes 319496 | tf_op jit(solution)/shard_map/ppermute | solution.py:60
  71.7 12.0 %collective-permute-start.14 = (bf16[1,208,256]{2,1,0:T(8,128)(2,1)}, bf16[1,208,256]{2,1,0:T(8,128)(2,1)}, u32[]{:S(2)}, u32[]{:S(2)}) collective-permute-start(bf16[1,208,256]{2,1,0:T(8,128)(2,1)} %get-tuple-element.64), channel_id=1, source_target_pairs={{0,16},{1,17},{2,18},{3,19},{4,20},{5,21},{6,22},{7,23},{8,24},{9,... | collective-permute-start | bytes 319496 | tf_op jit(solution)/shard_map/ppermute | solution.py:60
  79.3 4.4 %collective-permute-start.15 = (bf16[1,208,256]{2,1,0:T(8,128)(2,1)}, bf16[1,208,256]{2,1,0:T(8,128)(2,1)}, u32[]{:S(2)}, u32[]{:S(2)}) collective-permute-start(bf16[1,208,256]{2,1,0:T(8,128)(2,1)} %get-tuple-element.63), channel_id=1, source_target_pairs={{0,24},{1,25},{2,26},{3,27},{4,28},{5,29},{6,30},{7,31},{8,0},{9,1... | collective-permute-start | bytes 319496 | tf_op jit(solution)/shard_map/ppermute | solution.py:60
  84.8 23.3 %collective-permute-start.22 = (bf16[4,208,256]{2,1,0:T(8,128)(2,1)S(1)}, bf16[4,208,256]{2,1,0:T(8,128)(2,1)S(1)}, u32[]{:S(2)}, u32[]{:S(2)}) collective-permute-start(bf16[4,208,256]{2,1,0:T(8,128)(2,1)S(1)} %pad_maximum_fusion.1.refs_0_), channel_id=1, source_target_pairs={{0,1},{1,0},{2,3},{3,2},{4,5},{5,4},{6,7},{7,6},{8,9},{9,8},{10,11... | collective-permute-start | bytes 1277960 | tf_op jit(solution)/shard_map/ppermute | solution.py:60
  86.7 21.4 %collective-permute-start.23 = (bf16[4,208,256]{2,1,0:T(8,128)(2,1)S(1)}, bf16[4,208,256]{2,1,0:T(8,128)(2,1)S(1)}, u32[]{:S(2)}, u32[]{:S(2)}) collective-permute-start(bf16[4,208,256]{2,1,0:T(8,128)(2,1)S(1)} %pad_maximum_fusion.1.refs_0_), channel_id=1, source_target_pairs={{0,6},{1,7},{2,0},{3,1},{4,2},{5,3},{6,4},{7,5},{8,14},{9,15},{10,... | collective-permute-start | bytes 1277960 | tf_op jit(solution)/shard_map/ppermute | solution.py:60
  89.7 18.5 %collective-permute-start.24 = (bf16[4,208,256]{2,1,0:T(8,128)(2,1)S(1)}, bf16[4,208,256]{2,1,0:T(8,128)(2,1)S(1)}, u32[]{:S(2)}, u32[]{:S(2)}) collective-permute-start(bf16[4,208,256]{2,1,0:T(8,128)(2,1)S(1)} %pad_maximum_fusion.1.refs_0_), channel_id=1, source_target_pairs={{0,4},{1,5},{2,6},{3,7},{4,0},{5,1},{6,2},{7,3},{8,12},{9,13},{10,... | collective-permute-start | bytes 1277960 | tf_op jit(solution)/shard_map/ppermute | solution.py:60
  90.3 21.7 %collective-permute-start.25 = (bf16[4,208,256]{2,1,0:T(8,128)(2,1)S(1)}, bf16[4,208,256]{2,1,0:T(8,128)(2,1)S(1)}, u32[]{:S(2)}, u32[]{:S(2)}) collective-permute-start(bf16[4,208,256]{2,1,0:T(8,128)(2,1)S(1)} %pad_maximum_fusion.1.refs_0_), channel_id=1, source_target_pairs={{0,2},{1,3},{2,4},{3,5},{4,6},{5,7},{6,0},{7,1},{8,10},{9,11},{10,... | collective-permute-start | bytes 1277960 | tf_op jit(solution)/shard_map/ppermute | solution.py:60
  112.0 1.9 %collective-permute-start.26 = (bf16[4,208,256]{2,1,0:T(8,128)(2,1)S(1)}, bf16[4,208,256]{2,1,0:T(8,128)(2,1)S(1)}, u32[]{:S(2)}, u32[]{:S(2)}) collective-permute-start(bf16[4,208,256]{2,1,0:T(8,128)(2,1)S(1)} %collective-permute-done.23.refs_1_), channel_id=1, source_target_pairs={{0,1},{1,0},{2,3},{3,2},{4,5},{5,4},{6,7},{7,6},{8,9},{9,8},{10,11... | collective-permute-start | bytes 1277960 | tf_op jit(solution)/shard_map/ppermute | solution.py:60
  112.5 2.0 %collective-permute-start.27 = (bf16[4,208,256]{2,1,0:T(8,128)(2,1)S(1)}, bf16[4,208,256]{2,1,0:T(8,128)(2,1)S(1)}, u32[]{:S(2)}, u32[]{:S(2)}) collective-permute-start(bf16[4,208,256]{2,1,0:T(8,128)(2,1)S(1)} %collective-permute-done.24.refs_2_), channel_id=1, source_target_pairs={{0,1},{1,0},{2,3},{3,2},{4,5},{5,4},{6,7},{7,6},{8,9},{9,8},{10,11... | collective-permute-start | bytes 1277960 | tf_op jit(solution)/shard_map/ppermute | solution.py:60
  112.5 2.6 %collective-permute-start.28 = (bf16[4,208,256]{2,1,0:T(8,128)(2,1)S(1)}, bf16[4,208,256]{2,1,0:T(8,128)(2,1)S(1)}, u32[]{:S(2)}, u32[]{:S(2)}) collective-permute-start(bf16[4,208,256]{2,1,0:T(8,128)(2,1)S(1)} %collective-permute-done.25.refs_3_), channel_id=1, source_target_pairs={{0,1},{1,0},{2,3},{3,2},{4,5},{5,4},{6,7},{7,6},{8,9},{9,8},{10,11... | collective-permute-start | bytes 1277960 | tf_op jit(solution)/shard_map/ppermute | solution.py:60
  129.7 4.5 %collective-permute-start.29 = (bf16[64,1024]{1,0:T(8,128)(2,1)S(1)}, bf16[64,1024]{1,0:T(8,128)(2,1)S(1)}, u32[]{:S(2)}, u32[]{:S(2)}) collective-permute-start(bf16[64,1024]{1,0:T(8,128)(2,1)S(1)} %get-tuple-element.55), channel_id=1, source_target_pairs={{0,24},{1,25},{2,26},{3,27},{4,28},{5,29},{6,30},{7,31},{8,0},{9,1... | collective-permute-start | bytes 393224 | tf_op jit(solution)/shard_map/ppermute | solution.py:60
  130.7 5.7 %collective-permute-start.30 = (bf16[64,1024]{1,0:T(8,128)(2,1)S(1)}, bf16[64,1024]{1,0:T(8,128)(2,1)S(1)}, u32[]{:S(2)}, u32[]{:S(2)}) collective-permute-start(bf16[64,1024]{1,0:T(8,128)(2,1)S(1)} %get-tuple-element.56), channel_id=1, source_target_pairs={{0,16},{1,17},{2,18},{3,19},{4,20},{5,21},{6,22},{7,23},{8,24},{9,... | collective-permute-start | bytes 393224 | tf_op jit(solution)/shard_map/ppermute | solution.py:60
  132.6 7.2 %collective-permute-start.31 = (bf16[64,1024]{1,0:T(8,128)(2,1)S(1)}, bf16[64,1024]{1,0:T(8,128)(2,1)S(1)}, u32[]{:S(2)}, u32[]{:S(2)}) collective-permute-start(bf16[64,1024]{1,0:T(8,128)(2,1)S(1)} %get-tuple-element.57), channel_id=1, source_target_pairs={{0,8},{1,9},{2,10},{3,11},{4,12},{5,13},{6,14},{7,15},{8,16},{9,17... | collective-permute-start | bytes 393224 | tf_op jit(solution)/shard_map/ppermute | solution.py:60
  (13 other events, 185.3 us)

commit v2 on v1

--- a/solution.py
+++ b/solution.py
@@ -30,7 +30,7 @@
 ROWS = GQ * R_DEV
 EXP_SCALE = HD ** (-0.5) * math.log2(math.e)
 FAR = 100
-STEP = 8
+STEP = 16
 PIECES = N_SEQ
 
 
@@ -437,13 +437,13 @@
     passage_out = encode(passage_q, passage_k, passage_v, 2, 1, passage_out)
     here0, passage_out = fence((here0, passage_out))
     mine0 = around_z(here0)
-    other0 = [swap(mine0[0])]
-    rel, other0 = fence((rel, other0))
+    passage_out = encode(passage_q, passage_k, passage_v, 3, 1, passage_out)
+    rel, passage_out = fence((rel, passage_out))
     here1 = across_x(choose(rel, second, near1))
-    passage_out = encode(passage_q, passage_k, passage_v, 3, 1, passage_out)
-    here1, passage_out = fence((here1, passage_out))
     mine1 = around_z(here1)
-    kv0 = mine0 + other0 + [swap(t) for t in mine0[1:]]
+    near, up, down = (swap(mine0[e]) for e in (0, 1, 3))
+    far = swap(mine0[2])
+    kv0 = mine0 + [near, up, far, down]
     state = read(0, kv0, q_arrays, ())
     other1 = [swap(mine1[0])]
     state, other1, far1 = fence((state, other1, mine1[1:]))

time: 141 us -> 131 us (0.929)
  waiting for transfers between devices: 47.3 us -> 39 us
  local copies, waits for them, and re-layouts: 4.51 us -> 0.09 us
  starting transfers between devices: 34.1 us -> 38.5 us
    ppermute x26, waiting for transfers between devices: 41.1 us -> 30.7 us  [shift_seq(): return lax.ppermute(a, 'seq', seq_pairs(dx, dz, dc))]
    unnamed x26 -> x6, local copies, waits for them, and re-layouts: 3.74 us -> 0.01 us
    ppermute x26, starting transfers between devices: 28.3 us -> 31.5 us  [shift_seq(): return lax.ppermute(a, 'seq', seq_pairs(dx, dz, dc))]
    ppermute x6, waiting for transfers between devices: 6.14 us -> 8.29 us  [shift_y(): return lax.ppermute(a, 'grp', [(i, (i + k) % N_GRP) for i in range(N_GRP)])]
  transfers between devices with their start and end apart: 32 -> 32, of which waited for: 14 -> 14; matrix products, arithmetic and copies ran while one was open for 2% -> 1% of each run, Pallas kernels for 24% -> 25%
where the time goes in v2:
time: 131 us
  Pallas kernels  49.4 us (38%)
  waiting for transfers between devices  39 us (30%)
  starting transfers between devices  38.5 us (29%)
  other arithmetic  2.3 us (2%)
  between operations  1.53 us (1%)
    ppermute x26, starting transfers between devices, shift_seq(): return lax.ppermute(a, 'seq', seq_pairs(dx, dz, dc))  31.5 us
    ppermute x26, waiting for transfers between devices, shift_seq(): return lax.ppermute(a, 'seq', seq_pairs(dx, dz, dc))  30.7 us
    pallas_call x2, Pallas kernels, read(): pl.pallas_call(functools.partial(reader_kernel, half), out_shape=(out,) *...  28.1 us
    pallas_call x3, Pallas kernels, encode(): pl.pallas_call(kernel, out_shape=jax.ShapeDtypeStruct((PLEN, HQ * HD), bf...  15.2 us
    ppermute x6, waiting for transfers between devices, shift_y(): return lax.ppermute(a, 'grp', [(i, (i + k) % N_GRP) for i in range(N_GRP)])  8.29 us
    ppermute x6, starting transfers between devices, shift_y(): return lax.ppermute(a, 'grp', [(i, (i + k) % N_GRP) for i in range(N_GRP)])  7 us
    pallas_call x2, Pallas kernels, pack(): pl.pallas_call(functools.partial(pack_kernel, half), out_shape=jax.ShapeD...  4.14 us
  transfers between devices with their start and end apart: 32, of which 14 were waited for; matrix products, arithmetic and copies ran while one was open for 1% of the time, Pallas kernels for 25%

profile of v2, /device:TPU:1, one launch (start us, length us, event | category | flops | bytes accessed | tf_op | source)
XLA Modules:
  0.0 130.8 jit_solution(16391829517610248789)
XLA Ops:
  0.6 2.1 %shard_map.105 = bf16[4,208,256]{2,1,0:T(8,128)(2,1)} custom-call(s32[1,4]{1,0:T(1,128)} %kept_ref.3, bf16[512,512]{1,0:T(8,128)(2,1)} %k_ref.9, bf16[512,512]{1,0:T(8,128)(2,1)} %v_ref.9), custom_call_target="tpu_custom_call" | custom-call | tf_op jit(solution)/shard_map/pallas_call | solution.py:95
  2.7 3.6 %collective-permute-start.3 = (bf16[4,208,256]{2,1,0:T(8,128)(2,1)}, bf16[4,208,256]{2,1,0:T(8,128)(2,1)S(1)}, u32[]{:S(2)}, u32[]{:S(2)}) collective-permute-start(bf16[4,208,256]{2,1,0:T(8,128)(2,1)} %shard_map.105), channel_id=1, source_target_pairs={{0,96},{32,0},{64,32},{96,64},{1,97},{33,1},{65,33},{97,65},{2,98}... | collective-permute-start | bytes 1277960 | tf_op jit(solution)/shard_map/ppermute | solution.py:47
  7.3 2.0 %queries.1 = (bf16[64,1536]{1,0:T(8,128)(2,1)}, bf16[64,1536]{1,0:T(8,128)(2,1)}, bf16[64,1536]{1,0:T(8,128)(2,1)}, bf16[64,1536]{1,0:T(8,128)(2,1)}) custom-call(s32[1,64]{1,0:T(1,128)} %pos_ref.1, bf16[64,4096]{1,0:T(8,128)(2,1)} %bitcast.10, bf16[64,512]{1,0:T(8,128)(2,1)} %bitcast.11, bf16[64,512]{1,0:T(8,128)(2,1)} %bitcast.12), custom_call_target="tpu_custom_call" | custom-call | tf_op jit(solution)/shard_map/queries/pallas_call | solution.py:125
  9.3 1.2 collective-permute-start
  10.6 2.5 %collective-permute-start.1 = (bf16[64,1536]{1,0:T(8,128)(2,1)}, bf16[64,1536]{1,0:T(8,128)(2,1)S(1)}, u32[]{:S(2)}, u32[]{:S(2)}) collective-permute-start(bf16[64,1536]{1,0:T(8,128)(2,1)} %get-tuple-element.30), channel_id=1, source_target_pairs={{0,16},{1,17},{2,18},{3,19},{4,20},{5,21},{6,22},{7,23},{8,24},{9,... | collective-permute-start | bytes 589832 | tf_op jit(solution)/shard_map/ppermute | solution.py:60
  13.8 2.1 %shard_map.108 = bf16[4,208,256]{2,1,0:T(8,128)(2,1)} custom-call(s32[1,4]{1,0:T(1,128)} %kept_ref.3, bf16[512,512]{1,0:T(8,128)(2,1)} %k_ref.9, bf16[512,512]{1,0:T(8,128)(2,1)} %v_ref.9), custom_call_target="tpu_custom_call" | custom-call | tf_op jit(solution)/shard_map/pallas_call | solution.py:95
  15.9 1.2 collective-permute-start.2
  17.1 6.5 %shard_map.104.rest_0_ = bf16[512,4096]{1,0:T(8,128)(2,1)} custom-call(bf16[512,4096]{1,0:T(8,128)(2,1)} %q_ref.5, bf16[512,512]{1,0:T(8,128)(2,1)} %k_ref.9, bf16[512,512]{1,0:T(8,128)(2,1)} %v_ref.9), custom_call_target="tpu_custom_call" | custom-call | flops 2147483648 | bytes 4718592 | tf_op jit(solution)/shard_map/pallas_call | solution.py:171
  23.6 2.1 %collective-permute-start.9 = (bf16[4,208,256]{2,1,0:T(8,128)(2,1)S(1)}, bf16[4,208,256]{2,1,0:T(8,128)(2,1)}, u32[]{:S(2)}, u32[]{:S(2)}) collective-permute-start(bf16[4,208,256]{2,1,0:T(8,128)(2,1)S(1)} %copy-done.2), channel_id=1, source_target_pairs={{0,96},{32,0},{64,32},{96,64},{1,97},{33,1},{65,33},{97,65},{2,98}... | collective-permute-start | bytes 1277960 | tf_op jit(solution)/shard_map/ppermute | solution.py:47
  25.6 3.2 %collective-permute-done.5 = bf16[4,208,256]{2,1,0:T(8,128)(2,1)S(1)} collective-permute-done((bf16[4,208,256]{2,1,0:T(8,128)(2,1)}, bf16[4,208,256]{2,1,0:T(8,128)(2,1)S(1)}, u32[]{:S(2)}, u32[]{:S(2)}) %collective-permute-start.5) | collective-permute-done | bytes 426016 | tf_op jit(solution)/shard_map/ppermute | solution.py:47
  29.0 2.5 %collective-permute-start.8 = (bf16[1,208,256]{2,1,0:T(8,128)(2,1)S(1)}, bf16[1,208,256]{2,1,0:T(8,128)(2,1)S(1)}, u32[]{:S(2)}, u32[]{:S(2)}) collective-permute-start(bf16[1,208,256]{2,1,0:T(8,128)(2,1)S(1)} %get-tuple-element.63), channel_id=1, source_target_pairs={{0,24},{1,25},{2,26},{3,27},{4,28},{5,29},{6,30},{7,31},{8,0},{9,1... | collective-permute-start | bytes 319496 | tf_op jit(solution)/shard_map/ppermute | solution.py:60
  33.2 1.2 collective-permute-start.6
  34.4 4.4 %shard_map.106.rest_0_ = bf16[512,4096]{1,0:T(8,128)(2,1)} custom-call(bf16[512,4096]{1,0:T(8,128)(2,1)} %q_ref.5, bf16[512,512]{1,0:T(8,128)(2,1)} %k_ref.9, bf16[512,512]{1,0:T(8,128)(2,1)} %v_ref.9, bf16[512,4096]{1,0:T(8,128)(2,1)} %shard_map.104.rest_0_), custom_call_target="tpu_custom_call", output_to_operand_aliasing={{}: (3, {})} | custom-call | flops 1073741824 | bytes 2359296 | tf_op jit(solution)/shard_map/pallas_call | solution.py:171
  38.8 1.2 collective-permute-done.6
  40.0 3.8 %collective-permute-start.15 = (bf16[4,208,256]{2,1,0:T(8,128)(2,1)S(1)}, bf16[4,208,256]{2,1,0:T(8,128)(2,1)S(1)}, u32[]{:S(2)}, u32[]{:S(2)}) collective-permute-start(bf16[4,208,256]{2,1,0:T(8,128)(2,1)S(1)} %pad_maximum_fusion.refs_0_), channel_id=1, source_target_pairs={{0,6},{1,7},{2,0},{3,1},{4,2},{5,3},{6,4},{7,5},{8,14},{9,15},{10,... | collective-permute-start | bytes 1277960 | tf_op jit(solution)/shard_map/ppermute | solution.py:60
  44.6 4.4 %shard_map.107 = bf16[512,4096]{1,0:T(8,128)(2,1)} custom-call(bf16[512,4096]{1,0:T(8,128)(2,1)} %q_ref.5, bf16[512,512]{1,0:T(8,128)(2,1)} %k_ref.9, bf16[512,512]{1,0:T(8,128)(2,1)} %v_ref.9, bf16[512,4096]{1,0:T(8,128)(2,1)} %shard_map.106.rest_0_), custom_call_target="tpu_custom_call", output_to_operand_aliasing={{}: (3, {})} | custom-call | flops 1073741824 | bytes 2359296 | tf_op jit(solution)/shard_map/pallas_call | solution.py:171
  48.9 5.1 %collective-permute-done.11 = bf16[4,208,256]{2,1,0:T(8,128)(2,1)} collective-permute-done((bf16[4,208,256]{2,1,0:T(8,128)(2,1)S(1)}, bf16[4,208,256]{2,1,0:T(8,128)(2,1)}, u32[]{:S(2)}, u32[]{:S(2)}) %collective-permute-start.11) | collective-permute-done | bytes 426016 | tf_op jit(solution)/shard_map/ppermute | solution.py:47
  54.0 1.2 select_select_fusion
  56.5 6.5 %collective-permute-start.19 = (bf16[4,208,256]{2,1,0:T(8,128)(2,1)S(1)}, bf16[4,208,256]{2,1,0:T(8,128)(2,1)S(1)}, u32[]{:S(2)}, u32[]{:S(2)}) collective-permute-start(bf16[4,208,256]{2,1,0:T(8,128)(2,1)S(1)} %collective-permute-done.15.refs_1_), channel_id=1, source_target_pairs={{0,1},{1,0},{2,3},{3,2},{4,5},{5,4},{6,7},{7,6},{8,9},{9,8},{10,11... | collective-permute-start | bytes 1277960 | tf_op jit(solution)/shard_map/ppermute | solution.py:60
  63.0 2.6 %collective-permute-done.17.refs_3_ = bf16[4,208,256]{2,1,0:T(8,128)(2,1)S(1)} collective-permute-done((bf16[4,208,256]{2,1,0:T(8,128)(2,1)S(1)}, bf16[4,208,256]{2,1,0:T(8,128)(2,1)S(1)}, u32[]{:S(2)}, u32[]{:S(2)}) %collective-permute-start.17) | collective-permute-done | bytes 426016 | tf_op jit(solution)/shard_map/ppermute | solution.py:60
  66.4 2.5 %collective-permute-start.13 = (bf16[1,208,256]{2,1,0:T(8,128)(2,1)S(1)}, bf16[1,208,256]{2,1,0:T(8,128)(2,1)S(1)}, u32[]{:S(2)}, u32[]{:S(2)}) collective-permute-start(bf16[1,208,256]{2,1,0:T(8,128)(2,1)S(1)} %get-tuple-element.60), channel_id=1, source_target_pairs={{0,16},{1,17},{2,18},{3,19},{4,20},{5,21},{6,22},{7,23},{8,24},{9,... | collective-permute-start | bytes 319496 | tf_op jit(solution)/shard_map/ppermute | solution.py:60
  68.9 3.6 %collective-permute-done.13 = bf16[1,208,256]{2,1,0:T(8,128)(2,1)S(1)} collective-permute-done((bf16[1,208,256]{2,1,0:T(8,128)(2,1)S(1)}, bf16[1,208,256]{2,1,0:T(8,128)(2,1)S(1)}, u32[]{:S(2)}, u32[]{:S(2)}) %collective-permute-start.13) | collective-permute-done | bytes 106528 | tf_op jit(solution)/shard_map/ppermute | solution.py:60
  72.5 4.8 %collective-permute-done.12 = bf16[1,208,256]{2,1,0:T(8,128)(2,1)S(1)} collective-permute-done((bf16[1,208,256]{2,1,0:T(8,128)(2,1)S(1)}, bf16[1,208,256]{2,1,0:T(8,128)(2,1)S(1)}, u32[]{:S(2)}, u32[]{:S(2)}) %collective-permute-start.12) | collective-permute-done | bytes 106528 | tf_op jit(solution)/shard_map/ppermute | solution.py:60
  77.3 2.1 %collective-permute-start.22 = (bf16[4,208,256]{2,1,0:T(8,128)(2,1)S(1)}, bf16[4,208,256]{2,1,0:T(8,128)(2,1)S(1)}, u32[]{:S(2)}, u32[]{:S(2)}) collective-permute-start(bf16[4,208,256]{2,1,0:T(8,128)(2,1)S(1)} %pad_maximum_fusion.1.refs_0_), channel_id=1, source_target_pairs={{0,1},{1,0},{2,3},{3,2},{4,5},{5,4},{6,7},{7,6},{8,9},{9,8},{10,11... | collective-permute-start | bytes 1277960 | tf_op jit(solution)/shard_map/ppermute | solution.py:60
  80.0 0.9 collective-permute-start.25
  80.9 13.7 %shard_map.109 = (f32[4,512,128]{2,1,0:T(8,128)S(1)}, f32[4,512,128]{2,1,0:T(8,128)S(1)}) custom-call(bf16[4,208,256]{2,1,0:T(8,128)(2,1)S(1)} %pad_maximum_fusion.refs_0_, bf16[4,208,256]{2,1,0:T(8,128)(2,1)S(1)} %collective-permute-done.15.refs_1_, bf16[4,208,256]{2,1,0:T(8,128)(2,1)S(1)} %collective-permute-done.16.refs_2_, ...), custom_call_target="tpu_custom_call" | custom-call | flops 5368709120 | bytes 8388608 | tf_op jit(solution)/shard_map/pallas_call | solution.py:365
  94.7 7.7 %collective-permute-done.25.refs_3_ = bf16[4,208,256]{2,1,0:T(8,128)(2,1)S(1)} collective-permute-done((bf16[4,208,256]{2,1,0:T(8,128)(2,1)S(1)}, bf16[4,208,256]{2,1,0:T(8,128)(2,1)S(1)}, u32[]{:S(2)}, u32[]{:S(2)}) %collective-permute-start.25) | collective-permute-done | bytes 426016 | tf_op jit(solution)/shard_map/ppermute | solution.py:60
  105.5 14.3 %shard_map.110 = (bf16[64,1024]{1,0:T(8,128)(2,1)S(1)}, bf16[64,1024]{1,0:T(8,128)(2,1)S(1)}, bf16[64,1024]{1,0:T(8,128)(2,1)S(1)}, bf16[64,1024]{1,0:T(8,128)(2,1)S(1)}) custom-call(bf16[4,208,256]{2,1,0:T(8,128)(2,1)S(1)} %pad_maximum_fusion.1.refs_0_, bf16[4,208,256]{2,1,0:T(8,128)(2,1)S(1)} %collective-permute-done.23.refs_1_, ...), custom_call_target="tpu_custom_call" | custom-call | flops 5368709120 | bytes 8388608 | tf_op jit(solution)/shard_map/pallas_call | solution.py:365
  120.2 1.0 collective-permute-start.30
  122.0 2.3 %collective-permute-done.29 = bf16[64,1024]{1,0:T(8,128)(2,1)S(1)} collective-permute-done((bf16[64,1024]{1,0:T(8,128)(2,1)S(1)}, bf16[64,1024]{1,0:T(8,128)(2,1)S(1)}, u32[]{:S(2)}, u32[]{:S(2)}) %collective-permute-start.29) | collective-permute-done | bytes 131104 | tf_op jit(solution)/shard_map/ppermute | solution.py:60
  124.3 1.6 %collective-permute-done.30 = bf16[64,1024]{1,0:T(8,128)(2,1)S(1)} collective-permute-done((bf16[64,1024]{1,0:T(8,128)(2,1)S(1)}, bf16[64,1024]{1,0:T(8,128)(2,1)S(1)}, u32[]{:S(2)}, u32[]{:S(2)}) %collective-permute-start.30) | collective-permute-done | bytes 131104 | tf_op jit(solution)/shard_map/ppermute | solution.py:60
  125.9 4.0 %collective-permute-done.31 = bf16[64,1024]{1,0:T(8,128)(2,1)S(1)} collective-permute-done((bf16[64,1024]{1,0:T(8,128)(2,1)S(1)}, bf16[64,1024]{1,0:T(8,128)(2,1)S(1)}, u32[]{:S(2)}, u32[]{:S(2)}) %collective-permute-start.31) | collective-permute-done | bytes 131104 | tf_op jit(solution)/shard_map/ppermute | solution.py:60
  (54 shorter events, 11.6 us)
Async XLA Ops:
  2.7 22.9 %collective-permute-start.3 = (bf16[4,208,256]{2,1,0:T(8,128)(2,1)}, bf16[4,208,256]{2,1,0:T(8,128)(2,1)S(1)}, u32[]{:S(2)}, u32[]{:S(2)}) collective-permute-start(bf16[4,208,256]{2,1,0:T(8,128)(2,1)} %shard_map.105), channel_id=1, source_target_pairs={{0,96},{32,0},{64,32},{96,64},{1,97},{33,1},{65,33},{97,65},{2,98}... | collective-permute-start | bytes 1277960 | tf_op jit(solution)/shard_map/ppermute | solution.py:47
  6.3 19.4 %collective-permute-start.4 = (bf16[4,208,256]{2,1,0:T(8,128)(2,1)}, bf16[4,208,256]{2,1,0:T(8,128)(2,1)S(1)}, u32[]{:S(2)}, u32[]{:S(2)}) collective-permute-start(bf16[4,208,256]{2,1,0:T(8,128)(2,1)} %shard_map.105), channel_id=1, source_target_pairs={{0,64},{32,96},{64,0},{96,32},{1,65},{33,97},{65,1},{97,33},{2,66}... | collective-permute-start | bytes 1277960 | tf_op jit(solution)/shard_map/ppermute | solution.py:47
  6.6 22.2 %collective-permute-start.5 = (bf16[4,208,256]{2,1,0:T(8,128)(2,1)}, bf16[4,208,256]{2,1,0:T(8,128)(2,1)S(1)}, u32[]{:S(2)}, u32[]{:S(2)}) collective-permute-start(bf16[4,208,256]{2,1,0:T(8,128)(2,1)} %shard_map.105), channel_id=1, source_target_pairs={{0,32},{32,64},{64,96},{96,0},{1,33},{33,65},{65,97},{97,1},{2,34}... | collective-permute-start | bytes 1277960 | tf_op jit(solution)/shard_map/ppermute | solution.py:47
  9.3 6.5 %collective-permute-start = (bf16[64,1536]{1,0:T(8,128)(2,1)}, bf16[64,1536]{1,0:T(8,128)(2,1)S(1)}, u32[]{:S(2)}, u32[]{:S(2)}) collective-permute-start(bf16[64,1536]{1,0:T(8,128)(2,1)} %get-tuple-element.29), channel_id=1, source_target_pairs={{0,8},{1,9},{2,10},{3,11},{4,12},{5,13},{6,14},{7,15},{8,16},{9,17... | collective-permute-start | bytes 589832 | tf_op jit(solution)/shard_map/ppermute | solution.py:60
  10.6 13.0 %collective-permute-start.1 = (bf16[64,1536]{1,0:T(8,128)(2,1)}, bf16[64,1536]{1,0:T(8,128)(2,1)S(1)}, u32[]{:S(2)}, u32[]{:S(2)}) collective-permute-start(bf16[64,1536]{1,0:T(8,128)(2,1)} %get-tuple-element.30), channel_id=1, source_target_pairs={{0,16},{1,17},{2,18},{3,19},{4,20},{5,21},{6,22},{7,23},{8,24},{9,... | collective-permute-start | bytes 589832 | tf_op jit(solution)/shard_map/ppermute | solution.py:60
  15.9 9.8 %collective-permute-start.2 = (bf16[64,1536]{1,0:T(8,128)(2,1)}, bf16[64,1536]{1,0:T(8,128)(2,1)S(1)}, u32[]{:S(2)}, u32[]{:S(2)}) collective-permute-start(bf16[64,1536]{1,0:T(8,128)(2,1)} %get-tuple-element.31), channel_id=1, source_target_pairs={{0,24},{1,25},{2,26},{3,27},{4,28},{5,29},{6,30},{7,31},{8,0},{9,1... | collective-permute-start | bytes 589832 | tf_op jit(solution)/shard_map/ppermute | solution.py:60
  23.6 20.3 %collective-permute-start.9 = (bf16[4,208,256]{2,1,0:T(8,128)(2,1)S(1)}, bf16[4,208,256]{2,1,0:T(8,128)(2,1)}, u32[]{:S(2)}, u32[]{:S(2)}) collective-permute-start(bf16[4,208,256]{2,1,0:T(8,128)(2,1)S(1)} %copy-done.2), channel_id=1, source_target_pairs={{0,96},{32,0},{64,32},{96,64},{1,97},{33,1},{65,33},{97,65},{2,98}... | collective-permute-start | bytes 1277960 | tf_op jit(solution)/shard_map/ppermute | solution.py:47
  29.0 4.3 %collective-permute-start.8 = (bf16[1,208,256]{2,1,0:T(8,128)(2,1)S(1)}, bf16[1,208,256]{2,1,0:T(8,128)(2,1)S(1)}, u32[]{:S(2)}, u32[]{:S(2)}) collective-permute-start(bf16[1,208,256]{2,1,0:T(8,128)(2,1)S(1)} %get-tuple-element.63), channel_id=1, source_target_pairs={{0,24},{1,25},{2,26},{3,27},{4,28},{5,29},{6,30},{7,31},{8,0},{9,1... | collective-permute-start | bytes 319496 | tf_op jit(solution)/shard_map/ppermute | solution.py:60
  31.5 17.4 %collective-permute-start.10 = (bf16[4,208,256]{2,1,0:T(8,128)(2,1)S(1)}, bf16[4,208,256]{2,1,0:T(8,128)(2,1)S(1)}, u32[]{:S(2)}, u32[]{:S(2)}) collective-permute-start(bf16[4,208,256]{2,1,0:T(8,128)(2,1)S(1)} %copy-done.2), channel_id=1, source_target_pairs={{0,64},{32,96},{64,0},{96,32},{1,65},{33,97},{65,1},{97,33},{2,66}... | collective-permute-start | bytes 1277960 | tf_op jit(solution)/shard_map/ppermute | solution.py:47
  31.9 22.1 %collective-permute-start.11 = (bf16[4,208,256]{2,1,0:T(8,128)(2,1)S(1)}, bf16[4,208,256]{2,1,0:T(8,128)(2,1)}, u32[]{:S(2)}, u32[]{:S(2)}) collective-permute-start(bf16[4,208,256]{2,1,0:T(8,128)(2,1)S(1)} %copy-done.2), channel_id=1, source_target_pairs={{0,32},{32,64},{64,96},{96,0},{1,33},{33,65},{65,97},{97,1},{2,34}... | collective-permute-start | bytes 1277960 | tf_op jit(solution)/shard_map/ppermute | solution.py:47
  31.9 6.9 %collective-permute-start.7 = (bf16[1,208,256]{2,1,0:T(8,128)(2,1)S(1)}, bf16[1,208,256]{2,1,0:T(8,128)(2,1)S(1)}, u32[]{:S(2)}, u32[]{:S(2)}) collective-permute-start(bf16[1,208,256]{2,1,0:T(8,128)(2,1)S(1)} %get-tuple-element.64), channel_id=1, source_target_pairs={{0,16},{1,17},{2,18},{3,19},{4,20},{5,21},{6,22},{7,23},{8,24},{9,... | collective-permute-start | bytes 319496 | tf_op jit(solution)/shard_map/ppermute | solution.py:60
  33.2 6.7 %collective-permute-start.6 = (bf16[1,208,256]{2,1,0:T(8,128)(2,1)S(1)}, bf16[1,208,256]{2,1,0:T(8,128)(2,1)S(1)}, u32[]{:S(2)}, u32[]{:S(2)}) collective-permute-start(bf16[1,208,256]{2,1,0:T(8,128)(2,1)S(1)} %get-tuple-element.65), channel_id=1, source_target_pairs={{0,8},{1,9},{2,10},{3,11},{4,12},{5,13},{6,14},{7,15},{8,16},{9,17... | collective-permute-start | bytes 319496 | tf_op jit(solution)/shard_map/ppermute | solution.py:60
  40.0 16.5 %collective-permute-start.15 = (bf16[4,208,256]{2,1,0:T(8,128)(2,1)S(1)}, bf16[4,208,256]{2,1,0:T(8,128)(2,1)S(1)}, u32[]{:S(2)}, u32[]{:S(2)}) collective-permute-start(bf16[4,208,256]{2,1,0:T(8,128)(2,1)S(1)} %pad_maximum_fusion.refs_0_), channel_id=1, source_target_pairs={{0,6},{1,7},{2,0},{3,1},{4,2},{5,3},{6,4},{7,5},{8,14},{9,15},{10,... | collective-permute-start | bytes 1277960 | tf_op jit(solution)/shard_map/ppermute | solution.py:60
  43.9 19.2 %collective-permute-start.16 = (bf16[4,208,256]{2,1,0:T(8,128)(2,1)S(1)}, bf16[4,208,256]{2,1,0:T(8,128)(2,1)S(1)}, u32[]{:S(2)}, u32[]{:S(2)}) collective-permute-start(bf16[4,208,256]{2,1,0:T(8,128)(2,1)S(1)} %pad_maximum_fusion.refs_0_), channel_id=1, source_target_pairs={{0,4},{1,5},{2,6},{3,7},{4,0},{5,1},{6,2},{7,3},{8,12},{9,13},{10,... | collective-permute-start | bytes 1277960 | tf_op jit(solution)/shard_map/ppermute | solution.py:60
  43.9 21.8 %collective-permute-start.17 = (bf16[4,208,256]{2,1,0:T(8,128)(2,1)S(1)}, bf16[4,208,256]{2,1,0:T(8,128)(2,1)S(1)}, u32[]{:S(2)}, u32[]{:S(2)}) collective-permute-start(bf16[4,208,256]{2,1,0:T(8,128)(2,1)S(1)} %pad_maximum_fusion.refs_0_), channel_id=1, source_target_pairs={{0,2},{1,3},{2,4},{3,5},{4,6},{5,7},{6,0},{7,1},{8,10},{9,11},{10,... | collective-permute-start | bytes 1277960 | tf_op jit(solution)/shard_map/ppermute | solution.py:60
  55.3 11.2 %collective-permute-start.14 = (bf16[1,208,256]{2,1,0:T(8,128)(2,1)S(1)}, bf16[1,208,256]{2,1,0:T(8,128)(2,1)S(1)}, u32[]{:S(2)}, u32[]{:S(2)}) collective-permute-start(bf16[1,208,256]{2,1,0:T(8,128)(2,1)S(1)} %get-tuple-element.59), channel_id=1, source_target_pairs={{0,24},{1,25},{2,26},{3,27},{4,28},{5,29},{6,30},{7,31},{8,0},{9,1... | collective-permute-start | bytes 319496 | tf_op jit(solution)/shard_map/ppermute | solution.py:60
  55.7 23.6 %collective-permute-start.18 = (bf16[4,208,256]{2,1,0:T(8,128)(2,1)S(1)}, bf16[4,208,256]{2,1,0:T(8,128)(2,1)S(1)}, u32[]{:S(2)}, u32[]{:S(2)}) collective-permute-start(bf16[4,208,256]{2,1,0:T(8,128)(2,1)S(1)} %pad_maximum_fusion.refs_0_), channel_id=1, source_target_pairs={{0,1},{1,0},{2,3},{3,2},{4,5},{5,4},{6,7},{7,6},{8,9},{9,8},{10,11... | collective-permute-start | bytes 1277960 | tf_op jit(solution)/shard_map/ppermute | solution.py:60
  56.5 23.5 %collective-permute-start.19 = (bf16[4,208,256]{2,1,0:T(8,128)(2,1)S(1)}, bf16[4,208,256]{2,1,0:T(8,128)(2,1)S(1)}, u32[]{:S(2)}, u32[]{:S(2)}) collective-permute-start(bf16[4,208,256]{2,1,0:T(8,128)(2,1)S(1)} %collective-permute-done.15.refs_1_), channel_id=1, source_target_pairs={{0,1},{1,0},{2,3},{3,2},{4,5},{5,4},{6,7},{7,6},{8,9},{9,8},{10,11... | collective-permute-start | bytes 1277960 | tf_op jit(solution)/shard_map/ppermute | solution.py:60
  63.0 17.0 %collective-permute-start.20 = (bf16[4,208,256]{2,1,0:T(8,128)(2,1)S(1)}, bf16[4,208,256]{2,1,0:T(8,128)(2,1)S(1)}, u32[]{:S(2)}, u32[]{:S(2)}) collective-permute-start(bf16[4,208,256]{2,1,0:T(8,128)(2,1)S(1)} %collective-permute-done.16.refs_2_), channel_id=1, source_target_pairs={{0,1},{1,0},{2,3},{3,2},{4,5},{5,4},{6,7},{7,6},{8,9},{9,8},{10,11... | collective-permute-start | bytes 1277960 | tf_op jit(solution)/shard_map/ppermute | solution.py:60
  65.7 15.3 %collective-permute-start.21 = (bf16[4,208,256]{2,1,0:T(8,128)(2,1)S(1)}, bf16[4,208,256]{2,1,0:T(8,128)(2,1)S(1)}, u32[]{:S(2)}, u32[]{:S(2)}) collective-permute-start(bf16[4,208,256]{2,1,0:T(8,128)(2,1)S(1)} %collective-permute-done.17.refs_3_), channel_id=1, source_target_pairs={{0,1},{1,0},{2,3},{3,2},{4,5},{5,4},{6,7},{7,6},{8,9},{9,8},{10,11... | collective-permute-start | bytes 1277960 | tf_op jit(solution)/shard_map/ppermute | solution.py:60
  66.4 6.0 %collective-permute-start.13 = (bf16[1,208,256]{2,1,0:T(8,128)(2,1)S(1)}, bf16[1,208,256]{2,1,0:T(8,128)(2,1)S(1)}, u32[]{:S(2)}, u32[]{:S(2)}) collective-permute-start(bf16[1,208,256]{2,1,0:T(8,128)(2,1)S(1)} %get-tuple-element.60), channel_id=1, source_target_pairs={{0,16},{1,17},{2,18},{3,19},{4,20},{5,21},{6,22},{7,23},{8,24},{9,... | collective-permute-start | bytes 319496 | tf_op jit(solution)/shard_map/ppermute | solution.py:60
  72.5 4.8 %collective-permute-start.12 = (bf16[1,208,256]{2,1,0:T(8,128)(2,1)S(1)}, bf16[1,208,256]{2,1,0:T(8,128)(2,1)S(1)}, u32[]{:S(2)}, u32[]{:S(2)}) collective-permute-start(bf16[1,208,256]{2,1,0:T(8,128)(2,1)S(1)} %get-tuple-element.61), channel_id=1, source_target_pairs={{0,8},{1,9},{2,10},{3,11},{4,12},{5,13},{6,14},{7,15},{8,16},{9,17... | collective-permute-start | bytes 319496 | tf_op jit(solution)/shard_map/ppermute | solution.py:60
  77.3 17.4 %collective-permute-start.22 = (bf16[4,208,256]{2,1,0:T(8,128)(2,1)S(1)}, bf16[4,208,256]{2,1,0:T(8,128)(2,1)S(1)}, u32[]{:S(2)}, u32[]{:S(2)}) collective-permute-start(bf16[4,208,256]{2,1,0:T(8,128)(2,1)S(1)} %pad_maximum_fusion.1.refs_0_), channel_id=1, source_target_pairs={{0,1},{1,0},{2,3},{3,2},{4,5},{5,4},{6,7},{7,6},{8,9},{9,8},{10,11... | collective-permute-start | bytes 1277960 | tf_op jit(solution)/shard_map/ppermute | solution.py:60
  79.4 15.3 %collective-permute-start.23 = (bf16[4,208,256]{2,1,0:T(8,128)(2,1)S(1)}, bf16[4,208,256]{2,1,0:T(8,128)(2,1)S(1)}, u32[]{:S(2)}, u32[]{:S(2)}) collective-permute-start(bf16[4,208,256]{2,1,0:T(8,128)(2,1)S(1)} %pad_maximum_fusion.1.refs_0_), channel_id=1, source_target_pairs={{0,6},{1,7},{2,0},{3,1},{4,2},{5,3},{6,4},{7,5},{8,14},{9,15},{10,... | collective-permute-start | bytes 1277960 | tf_op jit(solution)/shard_map/ppermute | solution.py:60
  80.0 14.7 %collective-permute-start.24 = (bf16[4,208,256]{2,1,0:T(8,128)(2,1)S(1)}, bf16[4,208,256]{2,1,0:T(8,128)(2,1)S(1)}, u32[]{:S(2)}, u32[]{:S(2)}) collective-permute-start(bf16[4,208,256]{2,1,0:T(8,128)(2,1)S(1)} %pad_maximum_fusion.1.refs_0_), channel_id=1, source_target_pairs={{0,4},{1,5},{2,6},{3,7},{4,0},{5,1},{6,2},{7,3},{8,12},{9,13},{10,... | collective-permute-start | bytes 1277960 | tf_op jit(solution)/shard_map/ppermute | solution.py:60
  80.0 22.4 %collective-permute-start.25 = (bf16[4,208,256]{2,1,0:T(8,128)(2,1)S(1)}, bf16[4,208,256]{2,1,0:T(8,128)(2,1)S(1)}, u32[]{:S(2)}, u32[]{:S(2)}) collective-permute-start(bf16[4,208,256]{2,1,0:T(8,128)(2,1)S(1)} %pad_maximum_fusion.1.refs_0_), channel_id=1, source_target_pairs={{0,2},{1,3},{2,4},{3,5},{4,6},{5,7},{6,0},{7,1},{8,10},{9,11},{10,... | collective-permute-start | bytes 1277960 | tf_op jit(solution)/shard_map/ppermute | solution.py:60
  102.4 1.9 %collective-permute-start.26 = (bf16[4,208,256]{2,1,0:T(8,128)(2,1)S(1)}, bf16[4,208,256]{2,1,0:T(8,128)(2,1)S(1)}, u32[]{:S(2)}, u32[]{:S(2)}) collective-permute-start(bf16[4,208,256]{2,1,0:T(8,128)(2,1)S(1)} %collective-permute-done.23.refs_1_), channel_id=1, source_target_pairs={{0,1},{1,0},{2,3},{3,2},{4,5},{5,4},{6,7},{7,6},{8,9},{9,8},{10,11... | collective-permute-start | bytes 1277960 | tf_op jit(solution)/shard_map/ppermute | solution.py:60
  102.9 2.0 %collective-permute-start.27 = (bf16[4,208,256]{2,1,0:T(8,128)(2,1)S(1)}, bf16[4,208,256]{2,1,0:T(8,128)(2,1)S(1)}, u32[]{:S(2)}, u32[]{:S(2)}) collective-permute-start(bf16[4,208,256]{2,1,0:T(8,128)(2,1)S(1)} %collective-permute-done.24.refs_2_), channel_id=1, source_target_pairs={{0,1},{1,0},{2,3},{3,2},{4,5},{5,4},{6,7},{7,6},{8,9},{9,8},{10,11... | collective-permute-start | bytes 1277960 | tf_op jit(solution)/shard_map/ppermute | solution.py:60
  102.9 2.6 %collective-permute-start.28 = (bf16[4,208,256]{2,1,0:T(8,128)(2,1)S(1)}, bf16[4,208,256]{2,1,0:T(8,128)(2,1)S(1)}, u32[]{:S(2)}, u32[]{:S(2)}) collective-permute-start(bf16[4,208,256]{2,1,0:T(8,128)(2,1)S(1)} %collective-permute-done.25.refs_3_), channel_id=1, source_target_pairs={{0,1},{1,0},{2,3},{3,2},{4,5},{5,4},{6,7},{7,6},{8,9},{9,8},{10,11... | collective-permute-start | bytes 1277960 | tf_op jit(solution)/shard_map/ppermute | solution.py:60
  119.8 4.5 %collective-permute-start.29 = (bf16[64,1024]{1,0:T(8,128)(2,1)S(1)}, bf16[64,1024]{1,0:T(8,128)(2,1)S(1)}, u32[]{:S(2)}, u32[]{:S(2)}) collective-permute-start(bf16[64,1024]{1,0:T(8,128)(2,1)S(1)} %get-tuple-element.51), channel_id=1, source_target_pairs={{0,24},{1,25},{2,26},{3,27},{4,28},{5,29},{6,30},{7,31},{8,0},{9,1... | collective-permute-start | bytes 393224 | tf_op jit(solution)/shard_map/ppermute | solution.py:60
  120.2 5.7 %collective-permute-start.30 = (bf16[64,1024]{1,0:T(8,128)(2,1)S(1)}, bf16[64,1024]{1,0:T(8,128)(2,1)S(1)}, u32[]{:S(2)}, u32[]{:S(2)}) collective-permute-start(bf16[64,1024]{1,0:T(8,128)(2,1)S(1)} %get-tuple-element.52), channel_id=1, source_target_pairs={{0,16},{1,17},{2,18},{3,19},{4,20},{5,21},{6,22},{7,23},{8,24},{9,... | collective-permute-start | bytes 393224 | tf_op jit(solution)/shard_map/ppermute | solution.py:60
  121.3 8.7 %collective-permute-start.31 = (bf16[64,1024]{1,0:T(8,128)(2,1)S(1)}, bf16[64,1024]{1,0:T(8,128)(2,1)S(1)}, u32[]{:S(2)}, u32[]{:S(2)}) collective-permute-start(bf16[64,1024]{1,0:T(8,128)(2,1)S(1)} %get-tuple-element.53), channel_id=1, source_target_pairs={{0,8},{1,9},{2,10},{3,11},{4,12},{5,13},{6,14},{7,15},{8,16},{9,17... | collective-permute-start | bytes 393224 | tf_op jit(solution)/shard_map/ppermute | solution.py:60
  (3 other events, 61.6 us)

commit v3 on v2

--- a/solution.py
+++ b/solution.py
@@ -65,7 +65,7 @@
     return s // (N_Z * 2), lax.rem(s // 2, N_Z), lax.rem(s, 2)
 
 
-def pack_kernel(half, kept_ref, k_ref, v_ref, out):
+def pack_kernel(half, kept_ref, k_ref, v_ref, out, k_rows, v_rows, sems):
     kept = [kept_ref[0, b] for b in range(NBLK)]
     before = [0]
     for b in range(NBLK):
@@ -73,17 +73,25 @@
     count = before[NBLK]
     row = lax.broadcasted_iota(jnp.int32, (16, HD), 0)
     meta = jnp.where(row == 0, count, FAR)
+    copies = []
     for j in range(KEEP):
         block = 0
         for b in range(NBLK):
             block = block + jnp.where((kept[b] > 0) & (before[b] == j), b, 0)
         meta = jnp.where(row == 1 + j, jnp.where(j < count, block, FAR), meta)
         start = pl.multiple_of(block * BLK + half * ROW, ROW)
+        copies.append(pltpu.make_async_copy(k_ref.at[pl.ds(start, ROW)], k_rows.at[j], sems.at[2 * j]))
+        copies.append(pltpu.make_async_copy(v_ref.at[pl.ds(start, ROW)], v_rows.at[j], sems.at[2 * j + 1]))
+        copies[-2].start()
+        copies[-1].start()
+    for copy in copies:
+        copy.wait()
+    for j in range(KEEP):
+        rows = slice(j * ROW, (j + 1) * ROW)
         for h in range(KVH):
             cols = slice(h * HD, (h + 1) * HD)
-            rows = slice(j * ROW, (j + 1) * ROW)
-            out[h, rows, :HD] = k_ref[pl.ds(start, ROW), cols]
-            out[h, rows, HD:] = v_ref[pl.ds(start, ROW), cols]
+            out[h, rows, :HD] = k_rows[j, :, cols]
+            out[h, rows, HD:] = v_rows[j, :, cols]
     meta = meta.astype(f32).astype(bf16)
     for h in range(KVH):
         out[h, META:, :HD] = meta
@@ -95,8 +103,14 @@
     return pl.pallas_call(
         functools.partial(pack_kernel, half),
         out_shape=jax.ShapeDtypeStruct((KVH, PIECE, KV2), bf16),
-        in_specs=[pl.BlockSpec(memory_space=pltpu.SMEM), vmem, vmem],
+        in_specs=[pl.BlockSpec(memory_space=pltpu.SMEM)] + [pl.BlockSpec(memory_space=pl.ANY)] * 2,
         out_specs=vmem,
+        scratch_shapes=[
+            pltpu.VMEM((KEEP, ROW, KVH * HD), bf16),
+            pltpu.VMEM((KEEP, ROW, KVH * HD), bf16),
+            pltpu.SemaphoreType.DMA((2 * KEEP,)),
+        ],
+        compiler_params=pltpu.CompilerParams(vmem_limit_bytes=60 << 20),
     )(kept, k, v)
 
 

time: 131 us -> 132 us (level)
  no operation moved by 1% of the time
where the time goes in v3:
time: 132 us
  Pallas kernels  50.4 us (38%)
  waiting for transfers between devices  39.1 us (30%)
  starting transfers between devices  38.1 us (29%)
  other arithmetic  2.3 us (2%)
  between operations  1.6 us (1%)
    ppermute x26, waiting for transfers between devices, shift_seq(): return lax.ppermute(a, 'seq', seq_pairs(dx, dz, dc))  31.8 us
    ppermute x26, starting transfers between devices, shift_seq(): return lax.ppermute(a, 'seq', seq_pairs(dx, dz, dc))  31 us
    pallas_call x2, Pallas kernels, read(): pl.pallas_call(functools.partial(reader_kernel, half), out_shape=(out,) *...  28.1 us
    pallas_call x3, Pallas kernels, encode(): pl.pallas_call(kernel, out_shape=jax.ShapeDtypeStruct((PLEN, HQ * HD), bf...  15.2 us
    ppermute x6, waiting for transfers between devices, shift_y(): return lax.ppermute(a, 'grp', [(i, (i + k) % N_GRP) for i in range(N_GRP)])  7.3 us
    ppermute x6, starting transfers between devices, shift_y(): return lax.ppermute(a, 'grp', [(i, (i + k) % N_GRP) for i in range(N_GRP)])  7.07 us
    pallas_call x2, Pallas kernels, pack(): pl.pallas_call(functools.partial(pack_kernel, half), out_shape=jax.ShapeD...  5.12 us
  transfers between devices with their start and end apart: 32, of which 14 were waited for; matrix products, arithmetic and copies ran while one was open for 1% of the time, Pallas kernels for 25%

profile of v3, /device:TPU:1, one launch (start us, length us, event | category | flops | bytes accessed | tf_op | source)
XLA Modules:
  0.0 131.6 jit_solution(6307748030950523064)
XLA Ops:
  0.6 2.6 %shard_map.105 = bf16[4,208,256]{2,1,0:T(8,128)(2,1)} custom-call(s32[1,4]{1,0:T(1,128)} %kept_ref.3, bf16[512,512]{1,0:T(8,128)(2,1)} %k_ref.9, bf16[512,512]{1,0:T(8,128)(2,1)} %v_ref.9), custom_call_target="tpu_custom_call" | custom-call | tf_op jit(solution)/shard_map/pallas_call | solution.py:103
  3.2 3.6 %collective-permute-start.3 = (bf16[4,208,256]{2,1,0:T(8,128)(2,1)}, bf16[4,208,256]{2,1,0:T(8,128)(2,1)S(1)}, u32[]{:S(2)}, u32[]{:S(2)}) collective-permute-start(bf16[4,208,256]{2,1,0:T(8,128)(2,1)} %shard_map.105), channel_id=1, source_target_pairs={{0,96},{32,0},{64,32},{96,64},{1,97},{33,1},{65,33},{97,65},{2,98}... | collective-permute-start | bytes 1277960 | tf_op jit(solution)/shard_map/ppermute | solution.py:47
  7.9 2.0 %queries.1 = (bf16[64,1536]{1,0:T(8,128)(2,1)}, bf16[64,1536]{1,0:T(8,128)(2,1)}, bf16[64,1536]{1,0:T(8,128)(2,1)}, bf16[64,1536]{1,0:T(8,128)(2,1)}) custom-call(s32[1,64]{1,0:T(1,128)} %pos_ref.1, bf16[64,4096]{1,0:T(8,128)(2,1)} %bitcast.10, bf16[64,512]{1,0:T(8,128)(2,1)} %bitcast.11, bf16[64,512]{1,0:T(8,128)(2,1)} %bitcast.12), custom_call_target="tpu_custom_call" | custom-call | tf_op jit(solution)/shard_map/queries/pallas_call | solution.py:139
  9.9 1.2 collective-permute-start
  11.1 2.5 %collective-permute-start.1 = (bf16[64,1536]{1,0:T(8,128)(2,1)}, bf16[64,1536]{1,0:T(8,128)(2,1)S(1)}, u32[]{:S(2)}, u32[]{:S(2)}) collective-permute-start(bf16[64,1536]{1,0:T(8,128)(2,1)} %get-tuple-element.30), channel_id=1, source_target_pairs={{0,16},{1,17},{2,18},{3,19},{4,20},{5,21},{6,22},{7,23},{8,24},{9,... | collective-permute-start | bytes 589832 | tf_op jit(solution)/shard_map/ppermute | solution.py:60
  14.3 2.6 %shard_map.108 = bf16[4,208,256]{2,1,0:T(8,128)(2,1)} custom-call(s32[1,4]{1,0:T(1,128)} %kept_ref.3, bf16[512,512]{1,0:T(8,128)(2,1)} %k_ref.9, bf16[512,512]{1,0:T(8,128)(2,1)} %v_ref.9), custom_call_target="tpu_custom_call" | custom-call | tf_op jit(solution)/shard_map/pallas_call | solution.py:103
  17.0 1.2 collective-permute-start.2
  18.2 6.5 %shard_map.104.rest_0_ = bf16[512,4096]{1,0:T(8,128)(2,1)} custom-call(bf16[512,4096]{1,0:T(8,128)(2,1)} %q_ref.5, bf16[512,512]{1,0:T(8,128)(2,1)} %k_ref.9, bf16[512,512]{1,0:T(8,128)(2,1)} %v_ref.9), custom_call_target="tpu_custom_call" | custom-call | flops 2147483648 | bytes 4718592 | tf_op jit(solution)/shard_map/pallas_call | solution.py:185
  24.7 2.1 %collective-permute-start.9 = (bf16[4,208,256]{2,1,0:T(8,128)(2,1)S(1)}, bf16[4,208,256]{2,1,0:T(8,128)(2,1)}, u32[]{:S(2)}, u32[]{:S(2)}) collective-permute-start(bf16[4,208,256]{2,1,0:T(8,128)(2,1)S(1)} %copy-done.2), channel_id=1, source_target_pairs={{0,96},{32,0},{64,32},{96,64},{1,97},{33,1},{65,33},{97,65},{2,98}... | collective-permute-start | bytes 1277960 | tf_op jit(solution)/shard_map/ppermute | solution.py:47
  26.7 2.7 %collective-permute-done.5 = bf16[4,208,256]{2,1,0:T(8,128)(2,1)S(1)} collective-permute-done((bf16[4,208,256]{2,1,0:T(8,128)(2,1)}, bf16[4,208,256]{2,1,0:T(8,128)(2,1)S(1)}, u32[]{:S(2)}, u32[]{:S(2)}) %collective-permute-start.5) | collective-permute-done | bytes 426016 | tf_op jit(solution)/shard_map/ppermute | solution.py:47
  29.5 2.5 %collective-permute-start.8 = (bf16[1,208,256]{2,1,0:T(8,128)(2,1)S(1)}, bf16[1,208,256]{2,1,0:T(8,128)(2,1)S(1)}, u32[]{:S(2)}, u32[]{:S(2)}) collective-permute-start(bf16[1,208,256]{2,1,0:T(8,128)(2,1)S(1)} %get-tuple-element.63), channel_id=1, source_target_pairs={{0,24},{1,25},{2,26},{3,27},{4,28},{5,29},{6,30},{7,31},{8,0},{9,1... | collective-permute-start | bytes 319496 | tf_op jit(solution)/shard_map/ppermute | solution.py:60
  33.8 1.2 collective-permute-start.6
  35.0 4.4 %shard_map.106.rest_0_ = bf16[512,4096]{1,0:T(8,128)(2,1)} custom-call(bf16[512,4096]{1,0:T(8,128)(2,1)} %q_ref.5, bf16[512,512]{1,0:T(8,128)(2,1)} %k_ref.9, bf16[512,512]{1,0:T(8,128)(2,1)} %v_ref.9, bf16[512,4096]{1,0:T(8,128)(2,1)} %shard_map.104.rest_0_), custom_call_target="tpu_custom_call", output_to_operand_aliasing={{}: (3, {})} | custom-call | flops 1073741824 | bytes 2359296 | tf_op jit(solution)/shard_map/pallas_call | solution.py:185
  39.3 1.6 %collective-permute-done.6 = bf16[1,208,256]{2,1,0:T(8,128)(2,1)S(1)} collective-permute-done((bf16[1,208,256]{2,1,0:T(8,128)(2,1)S(1)}, bf16[1,208,256]{2,1,0:T(8,128)(2,1)S(1)}, u32[]{:S(2)}, u32[]{:S(2)}) %collective-permute-start.6) | collective-permute-done | bytes 106528 | tf_op jit(solution)/shard_map/ppermute | solution.py:60
  41.0 3.8 %collective-permute-start.15 = (bf16[4,208,256]{2,1,0:T(8,128)(2,1)S(1)}, bf16[4,208,256]{2,1,0:T(8,128)(2,1)S(1)}, u32[]{:S(2)}, u32[]{:S(2)}) collective-permute-start(bf16[4,208,256]{2,1,0:T(8,128)(2,1)S(1)} %pad_maximum_fusion.refs_0_), channel_id=1, source_target_pairs={{0,6},{1,7},{2,0},{3,1},{4,2},{5,3},{6,4},{7,5},{8,14},{9,15},{10,... | collective-permute-start | bytes 1277960 | tf_op jit(solution)/shard_map/ppermute | solution.py:60
  45.6 4.4 %shard_map.107 = bf16[512,4096]{1,0:T(8,128)(2,1)} custom-call(bf16[512,4096]{1,0:T(8,128)(2,1)} %q_ref.5, bf16[512,512]{1,0:T(8,128)(2,1)} %k_ref.9, bf16[512,512]{1,0:T(8,128)(2,1)} %v_ref.9, bf16[512,4096]{1,0:T(8,128)(2,1)} %shard_map.106.rest_0_), custom_call_target="tpu_custom_call", output_to_operand_aliasing={{}: (3, {})} | custom-call | flops 1073741824 | bytes 2359296 | tf_op jit(solution)/shard_map/pallas_call | solution.py:185
  49.9 4.6 %collective-permute-done.11 = bf16[4,208,256]{2,1,0:T(8,128)(2,1)} collective-permute-done((bf16[4,208,256]{2,1,0:T(8,128)(2,1)S(1)}, bf16[4,208,256]{2,1,0:T(8,128)(2,1)}, u32[]{:S(2)}, u32[]{:S(2)}) %collective-permute-start.11) | collective-permute-done | bytes 426016 | tf_op jit(solution)/shard_map/ppermute | solution.py:47
  54.6 1.2 select_select_fusion
  57.1 6.9 %collective-permute-start.19 = (bf16[4,208,256]{2,1,0:T(8,128)(2,1)S(1)}, bf16[4,208,256]{2,1,0:T(8,128)(2,1)S(1)}, u32[]{:S(2)}, u32[]{:S(2)}) collective-permute-start(bf16[4,208,256]{2,1,0:T(8,128)(2,1)S(1)} %collective-permute-done.15.refs_1_), channel_id=1, source_target_pairs={{0,1},{1,0},{2,3},{3,2},{4,5},{5,4},{6,7},{7,6},{8,9},{9,8},{10,11... | collective-permute-start | bytes 1277960 | tf_op jit(solution)/shard_map/ppermute | solution.py:60
  64.0 2.6 %collective-permute-done.17.refs_3_ = bf16[4,208,256]{2,1,0:T(8,128)(2,1)S(1)} collective-permute-done((bf16[4,208,256]{2,1,0:T(8,128)(2,1)S(1)}, bf16[4,208,256]{2,1,0:T(8,128)(2,1)S(1)}, u32[]{:S(2)}, u32[]{:S(2)}) %collective-permute-start.17) | collective-permute-done | bytes 426016 | tf_op jit(solution)/shard_map/ppermute | solution.py:60
  67.4 2.1 %collective-permute-start.13 = (bf16[1,208,256]{2,1,0:T(8,128)(2,1)S(1)}, bf16[1,208,256]{2,1,0:T(8,128)(2,1)S(1)}, u32[]{:S(2)}, u32[]{:S(2)}) collective-permute-start(bf16[1,208,256]{2,1,0:T(8,128)(2,1)S(1)} %get-tuple-element.60), channel_id=1, source_target_pairs={{0,16},{1,17},{2,18},{3,19},{4,20},{5,21},{6,22},{7,23},{8,24},{9,... | collective-permute-start | bytes 319496 | tf_op jit(solution)/shard_map/ppermute | solution.py:60
  69.5 4.0 %collective-permute-done.13 = bf16[1,208,256]{2,1,0:T(8,128)(2,1)S(1)} collective-permute-done((bf16[1,208,256]{2,1,0:T(8,128)(2,1)S(1)}, bf16[1,208,256]{2,1,0:T(8,128)(2,1)S(1)}, u32[]{:S(2)}, u32[]{:S(2)}) %collective-permute-start.13) | collective-permute-done | bytes 106528 | tf_op jit(solution)/shard_map/ppermute | solution.py:60
  73.5 4.8 %collective-permute-done.12 = bf16[1,208,256]{2,1,0:T(8,128)(2,1)S(1)} collective-permute-done((bf16[1,208,256]{2,1,0:T(8,128)(2,1)S(1)}, bf16[1,208,256]{2,1,0:T(8,128)(2,1)S(1)}, u32[]{:S(2)}, u32[]{:S(2)}) %collective-permute-start.12) | collective-permute-done | bytes 106528 | tf_op jit(solution)/shard_map/ppermute | solution.py:60
  78.3 2.1 %collective-permute-start.22 = (bf16[4,208,256]{2,1,0:T(8,128)(2,1)S(1)}, bf16[4,208,256]{2,1,0:T(8,128)(2,1)S(1)}, u32[]{:S(2)}, u32[]{:S(2)}) collective-permute-start(bf16[4,208,256]{2,1,0:T(8,128)(2,1)S(1)} %pad_maximum_fusion.1.refs_0_), channel_id=1, source_target_pairs={{0,1},{1,0},{2,3},{3,2},{4,5},{5,4},{6,7},{7,6},{8,9},{9,8},{10,11... | collective-permute-start | bytes 1277960 | tf_op jit(solution)/shard_map/ppermute | solution.py:60
  81.0 0.9 collective-permute-start.25
  81.9 13.7 %shard_map.109 = (f32[4,512,128]{2,1,0:T(8,128)S(1)}, f32[4,512,128]{2,1,0:T(8,128)S(1)}) custom-call(bf16[4,208,256]{2,1,0:T(8,128)(2,1)S(1)} %pad_maximum_fusion.refs_0_, bf16[4,208,256]{2,1,0:T(8,128)(2,1)S(1)} %collective-permute-done.15.refs_1_, bf16[4,208,256]{2,1,0:T(8,128)(2,1)S(1)} %collective-permute-done.16.refs_2_, ...), custom_call_target="tpu_custom_call" | custom-call | flops 5368709120 | bytes 8388608 | tf_op jit(solution)/shard_map/pallas_call | solution.py:379
  95.7 7.7 %collective-permute-done.25.refs_3_ = bf16[4,208,256]{2,1,0:T(8,128)(2,1)S(1)} collective-permute-done((bf16[4,208,256]{2,1,0:T(8,128)(2,1)S(1)}, bf16[4,208,256]{2,1,0:T(8,128)(2,1)S(1)}, u32[]{:S(2)}, u32[]{:S(2)}) %collective-permute-start.25) | collective-permute-done | bytes 426016 | tf_op jit(solution)/shard_map/ppermute | solution.py:60
  106.5 14.3 %shard_map.110 = (bf16[64,1024]{1,0:T(8,128)(2,1)S(1)}, bf16[64,1024]{1,0:T(8,128)(2,1)S(1)}, bf16[64,1024]{1,0:T(8,128)(2,1)S(1)}, bf16[64,1024]{1,0:T(8,128)(2,1)S(1)}) custom-call(bf16[4,208,256]{2,1,0:T(8,128)(2,1)S(1)} %pad_maximum_fusion.1.refs_0_, bf16[4,208,256]{2,1,0:T(8,128)(2,1)S(1)} %collective-permute-done.23.refs_1_, ...), custom_call_target="tpu_custom_call" | custom-call | flops 5368709120 | bytes 8388608 | tf_op jit(solution)/shard_map/pallas_call | solution.py:379
  120.9 0.9 collective-permute-start.30
  122.6 2.7 %collective-permute-done.29 = bf16[64,1024]{1,0:T(8,128)(2,1)S(1)} collective-permute-done((bf16[64,1024]{1,0:T(8,128)(2,1)S(1)}, bf16[64,1024]{1,0:T(8,128)(2,1)S(1)}, u32[]{:S(2)}, u32[]{:S(2)}) %collective-permute-start.29) | collective-permute-done | bytes 131104 | tf_op jit(solution)/shard_map/ppermute | solution.py:60
  125.3 1.6 %collective-permute-done.30 = bf16[64,1024]{1,0:T(8,128)(2,1)S(1)} collective-permute-done((bf16[64,1024]{1,0:T(8,128)(2,1)S(1)}, bf16[64,1024]{1,0:T(8,128)(2,1)S(1)}, u32[]{:S(2)}, u32[]{:S(2)}) %collective-permute-start.30) | collective-permute-done | bytes 131104 | tf_op jit(solution)/shard_map/ppermute | solution.py:60
  126.9 3.8 %collective-permute-done.31 = bf16[64,1024]{1,0:T(8,128)(2,1)S(1)} collective-permute-done((bf16[64,1024]{1,0:T(8,128)(2,1)S(1)}, bf16[64,1024]{1,0:T(8,128)(2,1)S(1)}, u32[]{:S(2)}, u32[]{:S(2)}) %collective-permute-start.31) | collective-permute-done | bytes 131104 | tf_op jit(solution)/shard_map/ppermute | solution.py:60
  (54 shorter events, 11.3 us)
Async XLA Ops:
  3.2 23.5 %collective-permute-start.3 = (bf16[4,208,256]{2,1,0:T(8,128)(2,1)}, bf16[4,208,256]{2,1,0:T(8,128)(2,1)S(1)}, u32[]{:S(2)}, u32[]{:S(2)}) collective-permute-start(bf16[4,208,256]{2,1,0:T(8,128)(2,1)} %shard_map.105), channel_id=1, source_target_pairs={{0,96},{32,0},{64,32},{96,64},{1,97},{33,1},{65,33},{97,65},{2,98}... | collective-permute-start | bytes 1277960 | tf_op jit(solution)/shard_map/ppermute | solution.py:47
  6.8 19.9 %collective-permute-start.4 = (bf16[4,208,256]{2,1,0:T(8,128)(2,1)}, bf16[4,208,256]{2,1,0:T(8,128)(2,1)S(1)}, u32[]{:S(2)}, u32[]{:S(2)}) collective-permute-start(bf16[4,208,256]{2,1,0:T(8,128)(2,1)} %shard_map.105), channel_id=1, source_target_pairs={{0,64},{32,96},{64,0},{96,32},{1,65},{33,97},{65,1},{97,33},{2,66}... | collective-permute-start | bytes 1277960 | tf_op jit(solution)/shard_map/ppermute | solution.py:47
  7.2 22.2 %collective-permute-start.5 = (bf16[4,208,256]{2,1,0:T(8,128)(2,1)}, bf16[4,208,256]{2,1,0:T(8,128)(2,1)S(1)}, u32[]{:S(2)}, u32[]{:S(2)}) collective-permute-start(bf16[4,208,256]{2,1,0:T(8,128)(2,1)} %shard_map.105), channel_id=1, source_target_pairs={{0,32},{32,64},{64,96},{96,0},{1,33},{33,65},{65,97},{97,1},{2,34}... | collective-permute-start | bytes 1277960 | tf_op jit(solution)/shard_map/ppermute | solution.py:47
  9.9 7.0 %collective-permute-start = (bf16[64,1536]{1,0:T(8,128)(2,1)}, bf16[64,1536]{1,0:T(8,128)(2,1)S(1)}, u32[]{:S(2)}, u32[]{:S(2)}) collective-permute-start(bf16[64,1536]{1,0:T(8,128)(2,1)} %get-tuple-element.29), channel_id=1, source_target_pairs={{0,8},{1,9},{2,10},{3,11},{4,12},{5,13},{6,14},{7,15},{8,16},{9,17... | collective-permute-start | bytes 589832 | tf_op jit(solution)/shard_map/ppermute | solution.py:60
  11.1 13.5 %collective-permute-start.1 = (bf16[64,1536]{1,0:T(8,128)(2,1)}, bf16[64,1536]{1,0:T(8,128)(2,1)S(1)}, u32[]{:S(2)}, u32[]{:S(2)}) collective-permute-start(bf16[64,1536]{1,0:T(8,128)(2,1)} %get-tuple-element.30), channel_id=1, source_target_pairs={{0,16},{1,17},{2,18},{3,19},{4,20},{5,21},{6,22},{7,23},{8,24},{9,... | collective-permute-start | bytes 589832 | tf_op jit(solution)/shard_map/ppermute | solution.py:60
  17.0 9.8 %collective-permute-start.2 = (bf16[64,1536]{1,0:T(8,128)(2,1)}, bf16[64,1536]{1,0:T(8,128)(2,1)S(1)}, u32[]{:S(2)}, u32[]{:S(2)}) collective-permute-start(bf16[64,1536]{1,0:T(8,128)(2,1)} %get-tuple-element.31), channel_id=1, source_target_pairs={{0,24},{1,25},{2,26},{3,27},{4,28},{5,29},{6,30},{7,31},{8,0},{9,1... | collective-permute-start | bytes 589832 | tf_op jit(solution)/shard_map/ppermute | solution.py:60
  24.7 20.2 %collective-permute-start.9 = (bf16[4,208,256]{2,1,0:T(8,128)(2,1)S(1)}, bf16[4,208,256]{2,1,0:T(8,128)(2,1)}, u32[]{:S(2)}, u32[]{:S(2)}) collective-permute-start(bf16[4,208,256]{2,1,0:T(8,128)(2,1)S(1)} %copy-done.2), channel_id=1, source_target_pairs={{0,96},{32,0},{64,32},{96,64},{1,97},{33,1},{65,33},{97,65},{2,98}... | collective-permute-start | bytes 1277960 | tf_op jit(solution)/shard_map/ppermute | solution.py:47
  29.5 4.3 %collective-permute-start.8 = (bf16[1,208,256]{2,1,0:T(8,128)(2,1)S(1)}, bf16[1,208,256]{2,1,0:T(8,128)(2,1)S(1)}, u32[]{:S(2)}, u32[]{:S(2)}) collective-permute-start(bf16[1,208,256]{2,1,0:T(8,128)(2,1)S(1)} %get-tuple-element.63), channel_id=1, source_target_pairs={{0,24},{1,25},{2,26},{3,27},{4,28},{5,29},{6,30},{7,31},{8,0},{9,1... | collective-permute-start | bytes 319496 | tf_op jit(solution)/shard_map/ppermute | solution.py:60
  32.1 17.9 %collective-permute-start.10 = (bf16[4,208,256]{2,1,0:T(8,128)(2,1)S(1)}, bf16[4,208,256]{2,1,0:T(8,128)(2,1)S(1)}, u32[]{:S(2)}, u32[]{:S(2)}) collective-permute-start(bf16[4,208,256]{2,1,0:T(8,128)(2,1)S(1)} %copy-done.2), channel_id=1, source_target_pairs={{0,64},{32,96},{64,0},{96,32},{1,65},{33,97},{65,1},{97,33},{2,66}... | collective-permute-start | bytes 1277960 | tf_op jit(solution)/shard_map/ppermute | solution.py:47
  32.4 22.1 %collective-permute-start.11 = (bf16[4,208,256]{2,1,0:T(8,128)(2,1)S(1)}, bf16[4,208,256]{2,1,0:T(8,128)(2,1)}, u32[]{:S(2)}, u32[]{:S(2)}) collective-permute-start(bf16[4,208,256]{2,1,0:T(8,128)(2,1)S(1)} %copy-done.2), channel_id=1, source_target_pairs={{0,32},{32,64},{64,96},{96,0},{1,33},{33,65},{65,97},{97,1},{2,34}... | collective-permute-start | bytes 1277960 | tf_op jit(solution)/shard_map/ppermute | solution.py:47
  32.4 6.9 %collective-permute-start.7 = (bf16[1,208,256]{2,1,0:T(8,128)(2,1)S(1)}, bf16[1,208,256]{2,1,0:T(8,128)(2,1)S(1)}, u32[]{:S(2)}, u32[]{:S(2)}) collective-permute-start(bf16[1,208,256]{2,1,0:T(8,128)(2,1)S(1)} %get-tuple-element.64), channel_id=1, source_target_pairs={{0,16},{1,17},{2,18},{3,19},{4,20},{5,21},{6,22},{7,23},{8,24},{9,... | collective-permute-start | bytes 319496 | tf_op jit(solution)/shard_map/ppermute | solution.py:60
  33.8 7.2 %collective-permute-start.6 = (bf16[1,208,256]{2,1,0:T(8,128)(2,1)S(1)}, bf16[1,208,256]{2,1,0:T(8,128)(2,1)S(1)}, u32[]{:S(2)}, u32[]{:S(2)}) collective-permute-start(bf16[1,208,256]{2,1,0:T(8,128)(2,1)S(1)} %get-tuple-element.65), channel_id=1, source_target_pairs={{0,8},{1,9},{2,10},{3,11},{4,12},{5,13},{6,14},{7,15},{8,16},{9,17... | collective-permute-start | bytes 319496 | tf_op jit(solution)/shard_map/ppermute | solution.py:60
  41.0 16.1 %collective-permute-start.15 = (bf16[4,208,256]{2,1,0:T(8,128)(2,1)S(1)}, bf16[4,208,256]{2,1,0:T(8,128)(2,1)S(1)}, u32[]{:S(2)}, u32[]{:S(2)}) collective-permute-start(bf16[4,208,256]{2,1,0:T(8,128)(2,1)S(1)} %pad_maximum_fusion.refs_0_), channel_id=1, source_target_pairs={{0,6},{1,7},{2,0},{3,1},{4,2},{5,3},{6,4},{7,5},{8,14},{9,15},{10,... | collective-permute-start | bytes 1277960 | tf_op jit(solution)/shard_map/ppermute | solution.py:60
  44.8 19.2 %collective-permute-start.16 = (bf16[4,208,256]{2,1,0:T(8,128)(2,1)S(1)}, bf16[4,208,256]{2,1,0:T(8,128)(2,1)S(1)}, u32[]{:S(2)}, u32[]{:S(2)}) collective-permute-start(bf16[4,208,256]{2,1,0:T(8,128)(2,1)S(1)} %pad_maximum_fusion.refs_0_), channel_id=1, source_target_pairs={{0,4},{1,5},{2,6},{3,7},{4,0},{5,1},{6,2},{7,3},{8,12},{9,13},{10,... | collective-permute-start | bytes 1277960 | tf_op jit(solution)/shard_map/ppermute | solution.py:60
  44.8 21.8 %collective-permute-start.17 = (bf16[4,208,256]{2,1,0:T(8,128)(2,1)S(1)}, bf16[4,208,256]{2,1,0:T(8,128)(2,1)S(1)}, u32[]{:S(2)}, u32[]{:S(2)}) collective-permute-start(bf16[4,208,256]{2,1,0:T(8,128)(2,1)S(1)} %pad_maximum_fusion.refs_0_), channel_id=1, source_target_pairs={{0,2},{1,3},{2,4},{3,5},{4,6},{5,7},{6,0},{7,1},{8,10},{9,11},{10,... | collective-permute-start | bytes 1277960 | tf_op jit(solution)/shard_map/ppermute | solution.py:60
  55.8 11.6 %collective-permute-start.14 = (bf16[1,208,256]{2,1,0:T(8,128)(2,1)S(1)}, bf16[1,208,256]{2,1,0:T(8,128)(2,1)S(1)}, u32[]{:S(2)}, u32[]{:S(2)}) collective-permute-start(bf16[1,208,256]{2,1,0:T(8,128)(2,1)S(1)} %get-tuple-element.59), channel_id=1, source_target_pairs={{0,24},{1,25},{2,26},{3,27},{4,28},{5,29},{6,30},{7,31},{8,0},{9,1... | collective-permute-start | bytes 319496 | tf_op jit(solution)/shard_map/ppermute | solution.py:60
  56.3 24.1 %collective-permute-start.18 = (bf16[4,208,256]{2,1,0:T(8,128)(2,1)S(1)}, bf16[4,208,256]{2,1,0:T(8,128)(2,1)S(1)}, u32[]{:S(2)}, u32[]{:S(2)}) collective-permute-start(bf16[4,208,256]{2,1,0:T(8,128)(2,1)S(1)} %pad_maximum_fusion.refs_0_), channel_id=1, source_target_pairs={{0,1},{1,0},{2,3},{3,2},{4,5},{5,4},{6,7},{7,6},{8,9},{9,8},{10,11... | collective-permute-start | bytes 1277960 | tf_op jit(solution)/shard_map/ppermute | solution.py:60
  57.1 23.9 %collective-permute-start.19 = (bf16[4,208,256]{2,1,0:T(8,128)(2,1)S(1)}, bf16[4,208,256]{2,1,0:T(8,128)(2,1)S(1)}, u32[]{:S(2)}, u32[]{:S(2)}) collective-permute-start(bf16[4,208,256]{2,1,0:T(8,128)(2,1)S(1)} %collective-permute-done.15.refs_1_), channel_id=1, source_target_pairs={{0,1},{1,0},{2,3},{3,2},{4,5},{5,4},{6,7},{7,6},{8,9},{9,8},{10,11... | collective-permute-start | bytes 1277960 | tf_op jit(solution)/shard_map/ppermute | solution.py:60
  64.0 17.0 %collective-permute-start.20 = (bf16[4,208,256]{2,1,0:T(8,128)(2,1)S(1)}, bf16[4,208,256]{2,1,0:T(8,128)(2,1)S(1)}, u32[]{:S(2)}, u32[]{:S(2)}) collective-permute-start(bf16[4,208,256]{2,1,0:T(8,128)(2,1)S(1)} %collective-permute-done.16.refs_2_), channel_id=1, source_target_pairs={{0,1},{1,0},{2,3},{3,2},{4,5},{5,4},{6,7},{7,6},{8,9},{9,8},{10,11... | collective-permute-start | bytes 1277960 | tf_op jit(solution)/shard_map/ppermute | solution.py:60
  66.6 15.3 %collective-permute-start.21 = (bf16[4,208,256]{2,1,0:T(8,128)(2,1)S(1)}, bf16[4,208,256]{2,1,0:T(8,128)(2,1)S(1)}, u32[]{:S(2)}, u32[]{:S(2)}) collective-permute-start(bf16[4,208,256]{2,1,0:T(8,128)(2,1)S(1)} %collective-permute-done.17.refs_3_), channel_id=1, source_target_pairs={{0,1},{1,0},{2,3},{3,2},{4,5},{5,4},{6,7},{7,6},{8,9},{9,8},{10,11... | collective-permute-start | bytes 1277960 | tf_op jit(solution)/shard_map/ppermute | solution.py:60
  67.4 6.0 %collective-permute-start.13 = (bf16[1,208,256]{2,1,0:T(8,128)(2,1)S(1)}, bf16[1,208,256]{2,1,0:T(8,128)(2,1)S(1)}, u32[]{:S(2)}, u32[]{:S(2)}) collective-permute-start(bf16[1,208,256]{2,1,0:T(8,128)(2,1)S(1)} %get-tuple-element.60), channel_id=1, source_target_pairs={{0,16},{1,17},{2,18},{3,19},{4,20},{5,21},{6,22},{7,23},{8,24},{9,... | collective-permute-start | bytes 319496 | tf_op jit(solution)/shard_map/ppermute | solution.py:60
  73.5 4.8 %collective-permute-start.12 = (bf16[1,208,256]{2,1,0:T(8,128)(2,1)S(1)}, bf16[1,208,256]{2,1,0:T(8,128)(2,1)S(1)}, u32[]{:S(2)}, u32[]{:S(2)}) collective-permute-start(bf16[1,208,256]{2,1,0:T(8,128)(2,1)S(1)} %get-tuple-element.61), channel_id=1, source_target_pairs={{0,8},{1,9},{2,10},{3,11},{4,12},{5,13},{6,14},{7,15},{8,16},{9,17... | collective-permute-start | bytes 319496 | tf_op jit(solution)/shard_map/ppermute | solution.py:60
  78.3 17.4 %collective-permute-start.22 = (bf16[4,208,256]{2,1,0:T(8,128)(2,1)S(1)}, bf16[4,208,256]{2,1,0:T(8,128)(2,1)S(1)}, u32[]{:S(2)}, u32[]{:S(2)}) collective-permute-start(bf16[4,208,256]{2,1,0:T(8,128)(2,1)S(1)} %pad_maximum_fusion.1.refs_0_), channel_id=1, source_target_pairs={{0,1},{1,0},{2,3},{3,2},{4,5},{5,4},{6,7},{7,6},{8,9},{9,8},{10,11... | collective-permute-start | bytes 1277960 | tf_op jit(solution)/shard_map/ppermute | solution.py:60
  80.4 15.3 %collective-permute-start.23 = (bf16[4,208,256]{2,1,0:T(8,128)(2,1)S(1)}, bf16[4,208,256]{2,1,0:T(8,128)(2,1)S(1)}, u32[]{:S(2)}, u32[]{:S(2)}) collective-permute-start(bf16[4,208,256]{2,1,0:T(8,128)(2,1)S(1)} %pad_maximum_fusion.1.refs_0_), channel_id=1, source_target_pairs={{0,6},{1,7},{2,0},{3,1},{4,2},{5,3},{6,4},{7,5},{8,14},{9,15},{10,... | collective-permute-start | bytes 1277960 | tf_op jit(solution)/shard_map/ppermute | solution.py:60
  81.0 14.7 %collective-permute-start.24 = (bf16[4,208,256]{2,1,0:T(8,128)(2,1)S(1)}, bf16[4,208,256]{2,1,0:T(8,128)(2,1)S(1)}, u32[]{:S(2)}, u32[]{:S(2)}) collective-permute-start(bf16[4,208,256]{2,1,0:T(8,128)(2,1)S(1)} %pad_maximum_fusion.1.refs_0_), channel_id=1, source_target_pairs={{0,4},{1,5},{2,6},{3,7},{4,0},{5,1},{6,2},{7,3},{8,12},{9,13},{10,... | collective-permute-start | bytes 1277960 | tf_op jit(solution)/shard_map/ppermute | solution.py:60
  81.0 22.4 %collective-permute-start.25 = (bf16[4,208,256]{2,1,0:T(8,128)(2,1)S(1)}, bf16[4,208,256]{2,1,0:T(8,128)(2,1)S(1)}, u32[]{:S(2)}, u32[]{:S(2)}) collective-permute-start(bf16[4,208,256]{2,1,0:T(8,128)(2,1)S(1)} %pad_maximum_fusion.1.refs_0_), channel_id=1, source_target_pairs={{0,2},{1,3},{2,4},{3,5},{4,6},{5,7},{6,0},{7,1},{8,10},{9,11},{10,... | collective-permute-start | bytes 1277960 | tf_op jit(solution)/shard_map/ppermute | solution.py:60
  103.4 1.9 %collective-permute-start.26 = (bf16[4,208,256]{2,1,0:T(8,128)(2,1)S(1)}, bf16[4,208,256]{2,1,0:T(8,128)(2,1)S(1)}, u32[]{:S(2)}, u32[]{:S(2)}) collective-permute-start(bf16[4,208,256]{2,1,0:T(8,128)(2,1)S(1)} %collective-permute-done.23.refs_1_), channel_id=1, source_target_pairs={{0,1},{1,0},{2,3},{3,2},{4,5},{5,4},{6,7},{7,6},{8,9},{9,8},{10,11... | collective-permute-start | bytes 1277960 | tf_op jit(solution)/shard_map/ppermute | solution.py:60
  103.9 2.0 %collective-permute-start.27 = (bf16[4,208,256]{2,1,0:T(8,128)(2,1)S(1)}, bf16[4,208,256]{2,1,0:T(8,128)(2,1)S(1)}, u32[]{:S(2)}, u32[]{:S(2)}) collective-permute-start(bf16[4,208,256]{2,1,0:T(8,128)(2,1)S(1)} %collective-permute-done.24.refs_2_), channel_id=1, source_target_pairs={{0,1},{1,0},{2,3},{3,2},{4,5},{5,4},{6,7},{7,6},{8,9},{9,8},{10,11... | collective-permute-start | bytes 1277960 | tf_op jit(solution)/shard_map/ppermute | solution.py:60
  103.9 2.6 %collective-permute-start.28 = (bf16[4,208,256]{2,1,0:T(8,128)(2,1)S(1)}, bf16[4,208,256]{2,1,0:T(8,128)(2,1)S(1)}, u32[]{:S(2)}, u32[]{:S(2)}) collective-permute-start(bf16[4,208,256]{2,1,0:T(8,128)(2,1)S(1)} %collective-permute-done.25.refs_3_), channel_id=1, source_target_pairs={{0,1},{1,0},{2,3},{3,2},{4,5},{5,4},{6,7},{7,6},{8,9},{9,8},{10,11... | collective-permute-start | bytes 1277960 | tf_op jit(solution)/shard_map/ppermute | solution.py:60
  120.8 4.5 %collective-permute-start.29 = (bf16[64,1024]{1,0:T(8,128)(2,1)S(1)}, bf16[64,1024]{1,0:T(8,128)(2,1)S(1)}, u32[]{:S(2)}, u32[]{:S(2)}) collective-permute-start(bf16[64,1024]{1,0:T(8,128)(2,1)S(1)} %get-tuple-element.51), channel_id=1, source_target_pairs={{0,24},{1,25},{2,26},{3,27},{4,28},{5,29},{6,30},{7,31},{8,0},{9,1... | collective-permute-start | bytes 393224 | tf_op jit(solution)/shard_map/ppermute | solution.py:60
  120.9 6.0 %collective-permute-start.30 = (bf16[64,1024]{1,0:T(8,128)(2,1)S(1)}, bf16[64,1024]{1,0:T(8,128)(2,1)S(1)}, u32[]{:S(2)}, u32[]{:S(2)}) collective-permute-start(bf16[64,1024]{1,0:T(8,128)(2,1)S(1)} %get-tuple-element.52), channel_id=1, source_target_pairs={{0,16},{1,17},{2,18},{3,19},{4,20},{5,21},{6,22},{7,23},{8,24},{9,... | collective-permute-start | bytes 393224 | tf_op jit(solution)/shard_map/ppermute | solution.py:60
  121.8 8.9 %collective-permute-start.31 = (bf16[64,1024]{1,0:T(8,128)(2,1)S(1)}, bf16[64,1024]{1,0:T(8,128)(2,1)S(1)}, u32[]{:S(2)}, u32[]{:S(2)}) collective-permute-start(bf16[64,1024]{1,0:T(8,128)(2,1)S(1)} %get-tuple-element.53), channel_id=1, source_target_pairs={{0,8},{1,9},{2,10},{3,11},{4,12},{5,13},{6,14},{7,15},{8,16},{9,17... | collective-permute-start | bytes 393224 | tf_op jit(solution)/shard_map/ppermute | solution.py:60
  (3 other events, 61.1 us)
